TPU v7x, 32 devices: a whole 2x2x4 slice. The times are simulated.
32 devices in a mesh: fsdp: 8 (over y, x, core), seq: 4 (over z).
Axes of the slice: x: 2, y: 2, z: 4, core: 2. Of those that a mesh axis runs over, the one named last changes fastest.
Arguments:
- tokens: bfloat16 [12288, 1024], P(('fsdp', 'seq')), may hold values from -6 to 6
- segment_ids: int32 [12288], P(('fsdp', 'seq')), may hold values from -1 to 1, as said below
- ln1_gain: bfloat16 [1024], P('fsdp'), may hold values from 0.099609375 to 1.8984375
- ln1_bias: bfloat16 [1024], P('fsdp'), may hold values from -3 to 3
- w_qkv: bfloat16 [1024, 3072], P('fsdp'), may hold values from -0.1875 to 0.1875
- q_bias: bfloat16 [1024], P('fsdp'), may hold values from -3 to 3
- v_bias: bfloat16 [1024], P('fsdp'), may hold values from -3 to 3
- w_out: bfloat16 [1024, 1024], P('fsdp'), may hold values from -0.75 to 0.75
- out_bias: bfloat16 [1024], P('fsdp'), may hold values from -3 to 3
- ln2_gain: bfloat16 [1024], P('fsdp'), may hold values from 0.099609375 to 1.8984375
- ln2_bias: bfloat16 [1024], P('fsdp'), may hold values from -3 to 3
- w_fc1: bfloat16 [1024, 4096], P('fsdp'), may hold values from -0.1875 to 0.1875
- fc1_bias: bfloat16 [4096], P('fsdp'), may hold values from -3 to 3
- w_fc2: bfloat16 [4096, 1024], P('fsdp'), may hold values from -0.09375 to 0.09375
- fc2_bias: bfloat16 [1024], P('fsdp'), may hold values from -3 to 3
- cotangent: bfloat16 [12288, 1024], P(('fsdp', 'seq')), may hold values from -6 to 6
Outputs:
- layer_output: bfloat16 [12288, 1024], P(('fsdp', 'seq'))
- tokens_grad: float32 [12288, 1024], P(('fsdp', 'seq'))
- ln1_gain_grad: float32 [1024], P(('fsdp', 'seq'))
- ln1_bias_grad: float32 [1024], P(('fsdp', 'seq'))
- w_qkv_grad: float32 [1024, 3072], P('fsdp', 'seq')
- q_bias_grad: float32 [1024], P(('fsdp', 'seq'))
- v_bias_grad: float32 [1024], P(('fsdp', 'seq'))
- w_out_grad: float32 [1024, 1024], P('fsdp', 'seq')
- out_bias_grad: float32 [1024], P(('fsdp', 'seq'))
- ln2_gain_grad: float32 [1024], P(('fsdp', 'seq'))
- ln2_bias_grad: float32 [1024], P(('fsdp', 'seq'))
- w_fc1_grad: float32 [1024, 4096], P('fsdp', 'seq')
- fc1_bias_grad: float32 [4096], P(('fsdp', 'seq'))
- w_fc2_grad: float32 [4096, 1024], P('fsdp', 'seq')
- fc2_bias_grad: float32 [1024], P(('fsdp', 'seq'))
Inputs may be any that keep to these rules, and one draw needn't show every extreme that they name: `segment_ids`: each span of 1536 slots (one index of fsdp) holds whole images of 577 slots from its first slot on, numbered 0, 1, 2, ... within the span, then padding slots marked -1; every span holds at least half of 2 images and some span holds 2.
All inputs are finite; a program needn't handle non-finite values.
Results may differ from a plain program's by a relative error of at most 0.019.
Values may be sent and summed in bfloat16 or wider, within the bound.
No kernel may reach another device: no remote copies, remote signals or barrier semaphores. Data moves between devices by JAX's collectives and lax.ppermute only.
A program may use at most 192 MiB of HBM per device.

v0:
```python
from functools import partial

import jax
import jax.numpy as jnp
from jax import lax
from jax.sharding import PartitionSpec as P

HD = 64
LEN = 577


norm_eps = 1e-06
masked_score = -1000000000.0


def normalize(values, gain, shift):
    row_mean = jnp.mean(values, axis=-1, keepdims=True)
    centered = values - row_mean
    variance = jnp.mean(centered * centered, axis=-1, keepdims=True)
    return centered * lax.rsqrt(variance + norm_eps) * gain + shift


def contract_rows(left, right):
    return lax.dot_general(
        left, right, (((0,), (0,)), ((), ())), preferred_element_type=jnp.float32
    )


def times_transposed(left, right):
    return lax.dot_general(
        left, right, (((1,), (1,)), ((), ())), preferred_element_type=jnp.float32
    )


def column_sum(values):
    return jnp.sum(values, axis=0, dtype=jnp.float32)


def shards_per_block(row_count, seq_count):
    for factor in range(1, seq_count + 1):
        if seq_count % factor == 0 and (row_count * factor >= 512 or factor == seq_count):
            return factor
    return seq_count


def add_window(total, delta, start):
    current = lax.dynamic_slice_in_dim(total, start, delta.shape[0], 0)
    return lax.dynamic_update_slice_in_dim(total, current + delta, start, 0)


def shards(
    tokens,
    segment_ids,
    ln1_gain,
    ln1_bias,
    w_qkv,
    q_bias,
    v_bias,
    w_out,
    out_bias,
    ln2_gain,
    ln2_bias,
    w_fc1,
    fc1_bias,
    w_fc2,
    fc2_bias,
    cotangent,
):
    row_count = tokens.shape[0]
    feature_width = tokens.shape[1]
    seq_count = lax.axis_size("seq")
    span_rows = row_count * seq_count
    local_heads = feature_width // seq_count // HD
    block_rows = row_count * shards_per_block(row_count, seq_count)
    block_count = span_rows // block_rows
    margin = LEN - 1
    window = block_rows + 2 * margin
    offsets = jnp.arange(block_count, dtype=jnp.int32) * block_rows
    scale = HD ** (-0.5)
    as_float = jnp.float32

    def weight_grad(left, right):
        return contract_rows(left, right)

    attn_set = (
        lax.all_gather(ln1_gain, "fsdp", axis=0, tiled=True),
        lax.all_gather(ln1_bias, "fsdp", axis=0, tiled=True),
        lax.all_gather(w_qkv, "fsdp", axis=0, tiled=True),
        lax.all_gather(q_bias, "fsdp", axis=0, tiled=True),
        lax.all_gather(v_bias, "fsdp", axis=0, tiled=True),
        lax.all_gather(w_out, "fsdp", axis=0, tiled=True),
        lax.all_gather(out_bias, "fsdp", axis=0, tiled=True),
    )
    span_labels = lax.all_gather(segment_ids, "seq", axis=0, tiled=True)
    inputs = tokens.astype(as_float)
    gain_one = attn_set[0].astype(as_float)
    shift_one = attn_set[1].astype(as_float)
    first_norm = normalize(inputs, gain_one, shift_one).astype(jnp.bfloat16)
    projected = jnp.dot(first_norm, attn_set[2], preferred_element_type=as_float)
    bias_all = jnp.concatenate(
        [
            attn_set[3].astype(as_float),
            jnp.zeros((feature_width,), as_float),
            attn_set[4].astype(as_float),
        ]
    )
    packed = (projected + bias_all).astype(jnp.bfloat16).reshape(row_count, 3, feature_width)
    head_rows = lax.all_to_all(packed, "seq", split_axis=2, concat_axis=0, tiled=True)
    query_heads = head_rows[:, 0, :].reshape(span_rows, local_heads, HD)
    key_heads = head_rows[:, 1, :].reshape(span_rows, local_heads, HD)
    value_heads = head_rows[:, 2, :].reshape(span_rows, local_heads, HD)
    key_padded = jnp.pad(key_heads, ((margin, margin), (0, 0), (0, 0)))
    value_padded = jnp.pad(value_heads, ((margin, margin), (0, 0), (0, 0)))
    label_padded = jnp.pad(span_labels, (margin, margin), constant_values=-2)

    def block_scores(offset):
        query_block = lax.dynamic_slice_in_dim(query_heads, offset, block_rows, 0)
        label_block = lax.dynamic_slice_in_dim(span_labels, offset, block_rows, 0)
        key_window = lax.dynamic_slice_in_dim(key_padded, offset, window, 0)
        value_window = lax.dynamic_slice_in_dim(value_padded, offset, window, 0)
        label_window = lax.dynamic_slice_in_dim(label_padded, offset, window, 0)
        scaled = (
            jnp.einsum("qhd,khd->hqk", query_block, key_window, preferred_element_type=as_float)
            * scale
        )
        same_image = label_block[:, None] == label_window[None, :]
        return (
            query_block,
            key_window,
            value_window,
            jnp.where(same_image[None], scaled, masked_score),
        )

    def block_forward(offset):
        unused_query, unused_key, value_window, scores = block_scores(offset)
        row_peak = jnp.max(scores, axis=-1, keepdims=True)
        lifted = jnp.exp(scores - row_peak)
        row_total = jnp.sum(lifted, axis=-1, keepdims=True)
        attn_probs = (lifted / row_total).astype(jnp.bfloat16)
        block_out = jnp.einsum(
            "hqk,khd->qhd", attn_probs, value_window, preferred_element_type=as_float
        ).astype(jnp.bfloat16)
        return (block_out, (row_peak + jnp.log(row_total))[..., 0])

    head_out, log_totals = lax.map(block_forward, offsets)
    head_flat = head_out.reshape(span_rows, local_heads * HD)
    attended = lax.all_to_all(head_flat, "seq", split_axis=0, concat_axis=1, tiled=True)
    mixed = jnp.dot(attended, attn_set[5], preferred_element_type=as_float) + attn_set[6].astype(
        as_float
    )
    middle = inputs + mixed
    mlp_set = (
        lax.all_gather(ln2_gain, "fsdp", axis=0, tiled=True),
        lax.all_gather(ln2_bias, "fsdp", axis=0, tiled=True),
        lax.all_gather(w_fc1, "fsdp", axis=0, tiled=True),
        lax.all_gather(fc1_bias, "fsdp", axis=0, tiled=True),
        lax.all_gather(w_fc2, "fsdp", axis=0, tiled=True),
        lax.all_gather(fc2_bias, "fsdp", axis=0, tiled=True),
    )
    gain_two = mlp_set[0].astype(as_float)
    shift_two = mlp_set[1].astype(as_float)
    second_norm = normalize(middle, gain_two, shift_two).astype(jnp.bfloat16)
    hidden = jnp.dot(second_norm, mlp_set[2], preferred_element_type=as_float) + mlp_set[3].astype(
        as_float
    )
    activated = jax.nn.gelu(hidden, approximate=False).astype(jnp.bfloat16)
    branch = jnp.dot(activated, mlp_set[4], preferred_element_type=as_float) + mlp_set[5].astype(
        as_float
    )
    valid = (segment_ids >= 0).astype(as_float)[:, None]
    layer_output = (valid * (middle + branch)).astype(jnp.bfloat16)
    grad_out = valid * cotangent.astype(as_float)
    grad_branch = grad_out.astype(jnp.bfloat16)
    fc2_bias_part = column_sum(grad_branch)
    w_fc2_part = weight_grad(activated, grad_branch)
    grad_act = times_transposed(grad_branch, mlp_set[4])
    unused_hidden, gelu_back = jax.vjp(partial(jax.nn.gelu, approximate=False), hidden)
    grad_hidden = gelu_back(grad_act)[0].astype(jnp.bfloat16)
    fc1_bias_part = column_sum(grad_hidden)
    w_fc1_part = weight_grad(second_norm, grad_hidden)
    grad_norm_two = times_transposed(grad_hidden, mlp_set[2])
    unused_two, norm_two_back = jax.vjp(
        normalize, middle, mlp_set[0].astype(as_float), mlp_set[1].astype(as_float)
    )
    grad_mid_norm, ln2_gain_part, ln2_bias_part = norm_two_back(grad_norm_two)
    grad_middle = grad_out + grad_mid_norm
    grad_mixed = grad_middle.astype(jnp.bfloat16)
    out_bias_part = column_sum(grad_mixed)
    w_out_part = weight_grad(attended, grad_mixed)
    grad_attended = times_transposed(grad_mixed, attn_set[5]).astype(jnp.bfloat16)
    grad_heads = lax.all_to_all(
        grad_attended, "seq", split_axis=1, concat_axis=0, tiled=True
    ).reshape(span_rows, local_heads, HD)

    def block_backward(running, inputs_block):
        key_total, value_total = running
        offset, log_block = inputs_block
        query_block, key_window, value_window, scores = block_scores(offset)
        grad_block = lax.dynamic_slice_in_dim(grad_heads, offset, block_rows, 0)
        probs_full = jnp.exp(scores - log_block[..., None])
        attn_probs = probs_full.astype(jnp.bfloat16)
        value_delta = jnp.einsum(
            "hqk,qhd->khd", attn_probs, grad_block, preferred_element_type=as_float
        )
        grad_probs = jnp.einsum(
            "qhd,khd->hqk", grad_block, value_window, preferred_element_type=as_float
        )
        row_inner = jnp.sum(grad_probs * probs_full, axis=-1, keepdims=True)
        grad_scores = (probs_full * (grad_probs - row_inner)).astype(jnp.bfloat16)
        grad_query = (
            jnp.einsum("hqk,khd->qhd", grad_scores, key_window, preferred_element_type=as_float)
            * scale
        )
        key_delta = (
            jnp.einsum("hqk,qhd->khd", grad_scores, query_block, preferred_element_type=as_float)
            * scale
        )
        return (
            (
                add_window(key_total, key_delta, offset),
                add_window(value_total, value_delta, offset),
            ),
            grad_query,
        )

    zero_heads = jnp.zeros((span_rows + 2 * margin, local_heads, HD), as_float)
    (key_padded_grad, value_padded_grad), query_grad = lax.scan(
        block_backward, (zero_heads, zero_heads), (offsets, log_totals)
    )
    key_grad = key_padded_grad[margin : margin + span_rows]
    value_grad = value_padded_grad[margin : margin + span_rows]
    head_grads = jnp.concatenate(
        [
            query_grad.reshape(span_rows, 1, local_heads * HD),
            key_grad.reshape(span_rows, 1, local_heads * HD),
            value_grad.reshape(span_rows, 1, local_heads * HD),
        ],
        axis=1,
    ).astype(jnp.bfloat16)
    token_grads = lax.all_to_all(
        head_grads, "seq", split_axis=0, concat_axis=2, tiled=True
    ).reshape(row_count, 3 * feature_width)
    q_bias_part = column_sum(token_grads[:, :feature_width])
    v_bias_part = column_sum(token_grads[:, 2 * feature_width :])
    w_qkv_part = weight_grad(first_norm, token_grads)
    grad_norm_one = times_transposed(token_grads, attn_set[2])
    unused_one, norm_one_back = jax.vjp(
        normalize, inputs, attn_set[0].astype(as_float), attn_set[1].astype(as_float)
    )
    grad_input_norm, ln1_gain_part, ln1_bias_part = norm_one_back(grad_norm_one)
    tokens_grad = grad_middle + grad_input_norm
    partial_sums = (
        lax.psum_scatter(
            ln1_gain_part.astype(jnp.bfloat16), "fsdp", scatter_dimension=0, tiled=True
        ).astype(jnp.float32),
        lax.psum_scatter(
            ln1_bias_part.astype(jnp.bfloat16), "fsdp", scatter_dimension=0, tiled=True
        ).astype(jnp.float32),
        lax.psum_scatter(
            w_qkv_part.astype(jnp.bfloat16), "fsdp", scatter_dimension=0, tiled=True
        ).astype(jnp.float32),
        lax.psum_scatter(
            q_bias_part.astype(jnp.bfloat16), "fsdp", scatter_dimension=0, tiled=True
        ).astype(jnp.float32),
        lax.psum_scatter(
            v_bias_part.astype(jnp.bfloat16), "fsdp", scatter_dimension=0, tiled=True
        ).astype(jnp.float32),
        lax.psum_scatter(
            w_out_part.astype(jnp.bfloat16), "fsdp", scatter_dimension=0, tiled=True
        ).astype(jnp.float32),
        lax.psum_scatter(
            out_bias_part.astype(jnp.bfloat16), "fsdp", scatter_dimension=0, tiled=True
        ).astype(jnp.float32),
        lax.psum_scatter(
            ln2_gain_part.astype(jnp.bfloat16), "fsdp", scatter_dimension=0, tiled=True
        ).astype(jnp.float32),
        lax.psum_scatter(
            ln2_bias_part.astype(jnp.bfloat16), "fsdp", scatter_dimension=0, tiled=True
        ).astype(jnp.float32),
        lax.psum_scatter(
            w_fc1_part.astype(jnp.bfloat16), "fsdp", scatter_dimension=0, tiled=True
        ).astype(jnp.float32),
        lax.psum_scatter(
            fc1_bias_part.astype(jnp.bfloat16), "fsdp", scatter_dimension=0, tiled=True
        ).astype(jnp.float32),
        lax.psum_scatter(
            w_fc2_part.astype(jnp.bfloat16), "fsdp", scatter_dimension=0, tiled=True
        ).astype(jnp.float32),
        lax.psum_scatter(
            fc2_bias_part.astype(jnp.bfloat16), "fsdp", scatter_dimension=0, tiled=True
        ).astype(jnp.float32),
    )
    summed = (
        lax.psum_scatter(
            partial_sums[0].astype(jnp.bfloat16), "seq", scatter_dimension=0, tiled=True
        ).astype(jnp.float32),
        lax.psum_scatter(
            partial_sums[1].astype(jnp.bfloat16), "seq", scatter_dimension=0, tiled=True
        ).astype(jnp.float32),
        lax.psum_scatter(
            partial_sums[2].astype(jnp.bfloat16), "seq", scatter_dimension=1, tiled=True
        ).astype(jnp.float32),
        lax.psum_scatter(
            partial_sums[3].astype(jnp.bfloat16), "seq", scatter_dimension=0, tiled=True
        ).astype(jnp.float32),
        lax.psum_scatter(
            partial_sums[4].astype(jnp.bfloat16), "seq", scatter_dimension=0, tiled=True
        ).astype(jnp.float32),
        lax.psum_scatter(
            partial_sums[5].astype(jnp.bfloat16), "seq", scatter_dimension=1, tiled=True
        ).astype(jnp.float32),
        lax.psum_scatter(
            partial_sums[6].astype(jnp.bfloat16), "seq", scatter_dimension=0, tiled=True
        ).astype(jnp.float32),
        lax.psum_scatter(
            partial_sums[7].astype(jnp.bfloat16), "seq", scatter_dimension=0, tiled=True
        ).astype(jnp.float32),
        lax.psum_scatter(
            partial_sums[8].astype(jnp.bfloat16), "seq", scatter_dimension=0, tiled=True
        ).astype(jnp.float32),
        lax.psum_scatter(
            partial_sums[9].astype(jnp.bfloat16), "seq", scatter_dimension=1, tiled=True
        ).astype(jnp.float32),
        lax.psum_scatter(
            partial_sums[10].astype(jnp.bfloat16), "seq", scatter_dimension=0, tiled=True
        ).astype(jnp.float32),
        lax.psum_scatter(
            partial_sums[11].astype(jnp.bfloat16), "seq", scatter_dimension=1, tiled=True
        ).astype(jnp.float32),
        lax.psum_scatter(
            partial_sums[12].astype(jnp.bfloat16), "seq", scatter_dimension=0, tiled=True
        ).astype(jnp.float32),
    )
    return (
        layer_output,
        tokens_grad,
        summed[0],
        summed[1],
        summed[2],
        summed[3],
        summed[4],
        summed[5],
        summed[6],
        summed[7],
        summed[8],
        summed[9],
        summed[10],
        summed[11],
        summed[12],
    )


def solution(mesh):
    return jax.shard_map(
        shards,
        mesh=mesh,
        in_specs=(
            P(("fsdp", "seq"), None),
            P(("fsdp", "seq")),
            P("fsdp"),
            P("fsdp"),
            P("fsdp", None),
            P("fsdp"),
            P("fsdp"),
            P("fsdp", None),
            P("fsdp"),
            P("fsdp"),
            P("fsdp"),
            P("fsdp", None),
            P("fsdp"),
            P("fsdp", None),
            P("fsdp"),
            P(("fsdp", "seq"), None),
        ),
        out_specs=(
            P(("fsdp", "seq"), None),
            P(("fsdp", "seq"), None),
            P(("fsdp", "seq")),
            P(("fsdp", "seq")),
            P("fsdp", "seq"),
            P(("fsdp", "seq")),
            P(("fsdp", "seq")),
            P("fsdp", "seq"),
            P(("fsdp", "seq")),
            P(("fsdp", "seq")),
            P(("fsdp", "seq")),
            P("fsdp", "seq"),
            P(("fsdp", "seq")),
            P("fsdp", "seq"),
            P(("fsdp", "seq")),
        ),
        check_vma=False,
    )
```

profile of v0, /device:TPU:0, one launch (start us, length us, event | category | flops | bytes accessed | tf_op | source)
XLA Modules:
  0.0 857.7 jit_solution(11295137797014356997)
XLA Ops:
  77.1 75.7 %all-gather.4 = s32[4,1,384]{2,1,0:T(1,128)S(1)} all-gather(s32[1,1,384]{2,1,0:T(1,128)S(1)} %reshape.224), channel_id=1, replica_groups=mesh['fsdp'=8,'seq'=4] {'seq'}, dimensions={0}, use_global_device_ids=true | all-gather | bytes 7680 | tf_op jit(solution)/shard_map/all_gather | solution.py:94
  165.7 81.2 %while.26 = (s32[]{:T(128)}, bf16[2,768,4,64]{1,3,2,0:T(8,128)(2,1)}, f32[2,4,768]{2,1,0:T(4,128)S(1)}, s32[2]{0:T(128)S(1)}, bf16[2688,4,64]{0,2,1:T(8,128)(2,1...) while((s32[]{:T(128)}, ...), condition=%wide.region_5.6_spmd, body=%wide.region_2.5_spmd.sunk | while | flops 1582396416 | bytes 85851936 | solution.py:145
  170.6 12.1 %fusion.119 = (f32[4,768]{1,0:T(4,128)S(1)}, f32[4,768,1920]{2,1,0:T(8,128)}) fusion(pred[768,1920]{1,0:T(8,128)(4,1)S(1)} %broadcast_compare_fusion.4, bf16[2688,4,64]{0,2,1:T(8,128)(2,1)S(1)} %get-tuple-element.433, s32[]{:T(128)S(6)} %select_n.71, bf16[1536,4,64]{0,2,1:T(8,128)(2,1)} %get-tuple-element.432, s32[]{:T(128)S(6)} %select_n.72), kind=kOutput, calls=%fused_computation.3.clone.1 | convolution fusion | flops 772666368 | bytes 26456072 | tf_op jit(solution)/shard_map/while/body/eval_jaxpr/qhd,khd->hqk/dot_general | solution.py:123
  182.7 11.3 %fusion.120 = f32[4,768]{1,0:T(4,128)S(1)} fusion(f32[4,768,1920]{2,1,0:T(8,128)} %get-tuple-element.383, f32[4,768]{1,0:T(4,128)S(1)} %get-tuple-element.384, pred[768,1920]{1,0:T(8,128)(4,1)S(1)} %broadcast_compare_fusion.4), kind=kLoop, calls=%fused_computation.4.clone.1 | loop fusion | flops 23589888 | bytes 25092096 | tf_op jit(solution)/shard_map/while/body/eval_jaxpr/reduce_sum | solution.py:138
  193.9 11.6 %fusion.121 = bf16[2,768,4,64]{1,3,2,0:T(8,128)(2,1)S(1)} fusion(bf16[2,768,4,64]{1,3,2,0:T(8,128)(2,1)S(1)} %copy-done.17, s32[]{:T(128)S(6)} %copy.99, f32[4,768,1920]{2,1,0:T(8,128)} %get-tuple-element.383, f32[4,768]{1,0:T(4,128)S(1)} %fusion.120, f32[4,768]{1,0:T(4,128)S(1)} %get-tuple-element.384, ...), kind=kOutput, calls=%fused_computation.9.clone.1 | convolution fusion | flops 784662528 | bytes 26468360 | tf_op jit(solution)/shard_map/while/body/eval_jaxpr/hqk,khd->qhd/dot_general | solution.py:140
  211.3 11.9 %fusion.119 = (f32[4,768]{1,0:T(4,128)S(1)}, f32[4,768,1920]{2,1,0:T(8,128)}) fusion(pred[768,1920]{1,0:T(8,128)(4,1)S(1)} %broadcast_compare_fusion.4, bf16[2688,4,64]{0,2,1:T(8,128)(2,1)S(1)} %get-tuple-element.433, s32[]{:T(128)S(6)} %select_n.71, bf16[1536,4,64]{0,2,1:T(8,128)(2,1)} %get-tuple-element.432, s32[]{:T(128)S(6)} %select_n.72), kind=kOutput, calls=%fused_computation.3.clone.1 | convolution fusion | flops 772666368 | bytes 26456072 | tf_op jit(solution)/shard_map/while/body/eval_jaxpr/qhd,khd->hqk/dot_general | solution.py:123
  223.2 11.1 %fusion.120 = f32[4,768]{1,0:T(4,128)S(1)} fusion(f32[4,768,1920]{2,1,0:T(8,128)} %get-tuple-element.383, f32[4,768]{1,0:T(4,128)S(1)} %get-tuple-element.384, pred[768,1920]{1,0:T(8,128)(4,1)S(1)} %broadcast_compare_fusion.4), kind=kLoop, calls=%fused_computation.4.clone.1 | loop fusion | flops 23589888 | bytes 25092096 | tf_op jit(solution)/shard_map/while/body/eval_jaxpr/reduce_sum | solution.py:138
  234.3 11.7 %fusion.121 = bf16[2,768,4,64]{1,3,2,0:T(8,128)(2,1)S(1)} fusion(bf16[2,768,4,64]{1,3,2,0:T(8,128)(2,1)S(1)} %copy-done.17, s32[]{:T(128)S(6)} %copy.99, f32[4,768,1920]{2,1,0:T(8,128)} %get-tuple-element.383, f32[4,768]{1,0:T(4,128)S(1)} %fusion.120, f32[4,768]{1,0:T(4,128)S(1)} %get-tuple-element.384, ...), kind=kOutput, calls=%fused_computation.9.clone.1 | convolution fusion | flops 784662528 | bytes 26468360 | tf_op jit(solution)/shard_map/while/body/eval_jaxpr/hqk,khd->qhd/dot_general | solution.py:140
  298.5 20.9 %multiply_convert_fusion.1 = (bf16[384,4096]{1,0:T(8,128)(2,1)}, f32[384,4096]{1,0:T(8,128)}, f32[384,4096]{1,0:T(8,128)}) fusion(f32[4096]{0:T(1024)S(1)} %bitcast.133, bf16[1024,4096]{1,0:T(8,128)(2,1)} %all-gather.19.cloned.1.call-done, f32[384,1024]{1,0:T(8,128)} %copy-done.11, f32[1024]{0:T(1024)S(1)} %bitcast.142, f32[1024]{0:T(1024)S(1)} %bitcast.136, ...), kind=kOutput, calls=%fused_computation.56 | convolution fusion | flops 3327000576 | bytes 25717760 | tf_op jit(solution)/shard_map/dot_general | solution.py:163
  319.4 11.5 %fusion.81 = (bf16[4096]{0:T(1024)(128)(2,1)}, bf16[384,4096]{1,0:T(8,128)(2,1)S(1)}) fusion(f32[384,4096]{1,0:T(8,128)} %get-tuple-element.239, f32[384,4096]{1,0:T(8,128)} %get-tuple-element.250, bf16[4096,1024]{1,0:T(8,128)(2,1)} %all-gather.21.cloned.1.call-done, bf16[384,1024]{1,0:T(8,128)(2,1)} %param.35, f32[384]{0:T(512)S(1)} %compare_convert_fusion), kind=kOutput, calls=%fused_computation.137 | convolution fusion | flops 3245993984 | bytes 24913408 | tf_op jit(solution)/shard_map/dot_general | solution.py:30
  390.8 215.2 %while.27 = (s32[]{:T(128)}, f32[2688,4,64]{0,2,1:T(8,128)}, f32[2688,4,64]{0,2,1:T(8,128)}, bf16[2,768,4,64]{1,3,2,0:T(8,128)(2,1)}, s32[2]{0:T(128)S(1)}, /*in...) while((s32[]{:T(128)}, f32[2688,4,64]{0,2,1:T(8,128)}, ...), condition=%wide.region_12.13_spmd, body=%wide.region_10.12_spmd.sunk | while | flops 3866489856 | bytes 287363040 | solution.py:227
  395.2 13.9 %fusion.130 = f32[4,768,1920]{2,1,0:T(8,128)} fusion(bf16[2688,4,64]{0,2,1:T(8,128)(2,1)S(1)} %get-tuple-element.478, s32[]{:T(128)S(6)} %select_n.76, bf16[1536,4,64]{0,2,1:T(8,128)(2,1)} %get-tuple-element.475, s32[]{:T(128)S(6)} %select_n.77), kind=kOutput, calls=%fused_computation.37.clone.1 | convolution fusion | flops 754974720 | bytes 24969224 | tf_op jit(solution)/shard_map/while/body/eval_jaxpr/qhd,khd->hqk/dot_general | solution.py:123
  410.2 22.4 %multiply_reduce_fusion.5 = (f32[4,768]{1,0:T(4,128)S(1)}, f32[4,768,1920]{2,1,0:T(8,128)}) fusion(f32[4,768,1920]{2,1,0:T(8,128)} %fusion.130, f32[4,768]{1,0:T(4,128)S(1)} %dynamic-slice_bitcast_fusion.2, pred[768,1920]{1,0:T(8,128)(4,1)S(1)} %broadcast_compare_fusion.5, bf16[2688,4,64]{0,2,1:T(8,128)(2,1)S(1)} %get-tuple-element.481, ...), kind=kOutput, calls=%fused_computation.20.clone.1 | convolution fusion | flops 784462848 | bytes 50061320 | tf_op jit(solution)/shard_map/while/body/eval_jaxpr/qhd,khd->hqk/dot_general | solution.py:205
  432.6 17.8 %multiply_convert_fusion.4 = bf16[4,768,1920]{2,1,0:T(8,128)(2,1)S(1)} fusion(f32[4,768,1920]{2,1,0:T(8,128)} %get-tuple-element.397, f32[4,768,1920]{2,1,0:T(8,128)} %fusion.130, f32[4,768]{1,0:T(4,128)S(1)} %get-tuple-element.398, f32[4,768]{1,0:T(4,128)S(1)} %dynamic-slice_bitcast_fusion.2, pred[768,1920]{1,0:T(8,128)(4,1)S(1)} %broadcast_compare_fusion.5), kind=kLoop, calls=%fused_computation.19.clone.1 | loop fusion | flops 35389440 | bytes 60481536 | tf_op jit(solution)/shard_map/while/body/eval_jaxpr/convert_element_type | solution.py:209
  466.7 16.3 %fusion.132 = f32[1920,4,64]{0,2,1:T(8,128)S(1)} fusion(f32[4,768,1920]{2,1,0:T(8,128)} %fusion.130, f32[4,768]{1,0:T(4,128)S(1)} %dynamic-slice_bitcast_fusion.2, pred[768,1920]{1,0:T(8,128)(4,1)S(1)} %broadcast_compare_fusion.5, f32[2688,4,64]{0,2,1:T(8,128)} %get-tuple-element.456, s32[]{:T(128)S(6)} %select_n.76, ...), kind=kOutput, calls=%fused_computation.30.clone.1 | convolution fusion | flops 779059200 | bytes 29405192 | tf_op jit(solution)/shard_map/while/body/eval_jaxpr/hqk,qhd->khd/dot_general | solution.py:202
  506.6 12.7 %fusion.130 = f32[4,768,1920]{2,1,0:T(8,128)} fusion(bf16[2688,4,64]{0,2,1:T(8,128)(2,1)S(1)} %get-tuple-element.478, s32[]{:T(128)S(6)} %select_n.76, bf16[1536,4,64]{0,2,1:T(8,128)(2,1)} %get-tuple-element.475, s32[]{:T(128)S(6)} %select_n.77), kind=kOutput, calls=%fused_computation.37.clone.1 | convolution fusion | flops 754974720 | bytes 24969224 | tf_op jit(solution)/shard_map/while/body/eval_jaxpr/qhd,khd->hqk/dot_general | solution.py:123
  520.4 22.0 %multiply_reduce_fusion.5 = (f32[4,768]{1,0:T(4,128)S(1)}, f32[4,768,1920]{2,1,0:T(8,128)}) fusion(f32[4,768,1920]{2,1,0:T(8,128)} %fusion.130, f32[4,768]{1,0:T(4,128)S(1)} %dynamic-slice_bitcast_fusion.2, pred[768,1920]{1,0:T(8,128)(4,1)S(1)} %broadcast_compare_fusion.5, bf16[2688,4,64]{0,2,1:T(8,128)(2,1)S(1)} %get-tuple-element.481, ...), kind=kOutput, calls=%fused_computation.20.clone.1 | convolution fusion | flops 784462848 | bytes 50061320 | tf_op jit(solution)/shard_map/while/body/eval_jaxpr/qhd,khd->hqk/dot_general | solution.py:205
  542.3 17.0 %multiply_convert_fusion.4 = bf16[4,768,1920]{2,1,0:T(8,128)(2,1)S(1)} fusion(f32[4,768,1920]{2,1,0:T(8,128)} %get-tuple-element.397, f32[4,768,1920]{2,1,0:T(8,128)} %fusion.130, f32[4,768]{1,0:T(4,128)S(1)} %get-tuple-element.398, f32[4,768]{1,0:T(4,128)S(1)} %dynamic-slice_bitcast_fusion.2, pred[768,1920]{1,0:T(8,128)(4,1)S(1)} %broadcast_compare_fusion.5), kind=kLoop, calls=%fused_computation.19.clone.1 | loop fusion | flops 35389440 | bytes 60481536 | tf_op jit(solution)/shard_map/while/body/eval_jaxpr/convert_element_type | solution.py:209
  575.1 12.3 %fusion.132 = f32[1920,4,64]{0,2,1:T(8,128)S(1)} fusion(f32[4,768,1920]{2,1,0:T(8,128)} %fusion.130, f32[4,768]{1,0:T(4,128)S(1)} %dynamic-slice_bitcast_fusion.2, pred[768,1920]{1,0:T(8,128)(4,1)S(1)} %broadcast_compare_fusion.5, f32[2688,4,64]{0,2,1:T(8,128)} %get-tuple-element.456, s32[]{:T(128)S(6)} %select_n.76, ...), kind=kOutput, calls=%fused_computation.30.clone.1 | convolution fusion | flops 779059200 | bytes 29405192 | tf_op jit(solution)/shard_map/while/body/eval_jaxpr/hqk,qhd->khd/dot_general | solution.py:202
  622.4 73.3 %all-to-all-done.3 = bf16[1536,3,256]{2,1,0:T(4,128)(2,1)S(1)} async-done(((bf16[1536,3,256]{2,1,0:T(4,128)(2,1)}), bf16[1536,3,256]{2,1,0:T(4,128)(2,1)S(1)}, u32[]{:S(2)}, u32[]{:S(2)}) %all-to-all-start.3) | async-done | bytes 2359328 | tf_op jit(solution)/shard_map/all_to_all | solution.py:240
  738.3 28.8 %reduce-scatter.9.cloned.1.call-done = bf16[128,3072]{1,0:T(8,128)(2,1)} async-done(((bf16[1024,3072]{1,0:T(8,128)(2,1)}), bf16[128,3072]{1,0:T(8,128)(2,1)}) %reduce-scatter.9.cloned.1.call-update) | async-done | bytes 786448 | tf_op jit(solution)/shard_map/reduce_scatter | solution.py:259
  771.1 23.8 %all-reduce.21 = (bf16[1024]{0:T(1024)(128)(2,1)S(1)}, bf16[1024]{0:T(1024)(128)(2,1)S(1)}, bf16[1024]{0:T(1024)(128)(2,1)S(1)}, bf16[1024]{0:T(1024)(128)(2,1)S...) all-reduce(bf16[1024]{0:T(1024)(128)(2,1)S(1)} %get-tuple-element.1, ...), channel_id=2, replica_groups=mesh['fsdp'=8,'seq'=4] {'fsdp'}, use_global_device_ids=true, to_apply=%region_16.17.clone | all-reduce | flops 12288 | bytes 49152
  795.6 12.5 %all-reduce.22 = (bf16[128]{0:T(256)(128)(2,1)S(1)}, bf16[128]{0:T(256)(128)(2,1)S(1)}, bf16[128]{0:T(256)(128)(2,1)S(1)}, bf16[128]{0:T(256)(128)(2,1)S(1)}, bf...) all-reduce(bf16[128]{0:T(256)(128)(2,1)S(1)} %dynamic-slice.1, ...), channel_id=3, replica_groups=mesh['fsdp'=8,'seq'=4] {'seq'}, use_global_device_ids=true, to_apply=%region_17.18.clone | all-reduce | flops 1536 | bytes 6144
  826.6 22.4 %reduce-scatter.11.cloned.1.call-done = bf16[128,768]{1,0:T(8,128)(2,1)} async-done(((bf16[128,3072]{1,0:T(8,128)(2,1)}), bf16[128,768]{1,0:T(8,128)(2,1)}) %reduce-scatter.11.cloned.1.call-update) | async-done | bytes 196624 | tf_op jit(solution)/shard_map/reduce_scatter | solution.py:300
  (291 shorter events, 353.2 us)
Async XLA Ops:
  7.2 39.0 %copy-start.7 = (bf16[384,1024]{1,0:T(8,128)(2,1)S(1)}, bf16[384,1024]{1,0:T(8,128)(2,1)}, u32[]{:S(2)}) copy-start(bf16[384,1024]{1,0:T(8,128)(2,1)} %param.20) | copy-start | bytes 2359300
  7.2 51.0 %all-gather.15.cloned.1.call-start = ((), (), s32[]{:S(2)}) async-start(), calls=%async_computation.12 | async-start | bytes 7077888 | tf_op jit(solution)/shard_map/all_gather | solution.py:88
  7.9 286.0 %all-gather.17.cloned.1.call-start = ((), (), s32[]{:S(2)}) async-start(), calls=%async_computation.13 | async-start | bytes 2359296 | tf_op jit(solution)/shard_map/all_gather | solution.py:91
  8.7 289.8 %all-gather.19.cloned.1.call-start = ((), (), s32[]{:S(2)}) async-start(), calls=%async_computation.14 | async-start | bytes 9437184 | tf_op jit(solution)/shard_map/all_gather | solution.py:155
  71.8 81.2 %all-to-all-start = ((bf16[384,3,1024]{0,1,2:T(4,128)(2,1)}), bf16[384,3,1024]{0,1,2:T(4,128)(2,1)S(1)}, u32[]{:S(2)}, u32[]{:S(2)}) async-start(bf16[384,3,1024]{0,1,2:T(4,128)(2,1)} %copy.74), calls=%async_computation | async-start | bytes 6291456 | tf_op jit(solution)/shard_map/all_to_all | solution.py:108
  76.5 242.9 %all-gather.21.cloned.1.call-start = ((), (), s32[]{:S(2)}) async-start(), calls=%async_computation.15 | async-start | bytes 9437184 | tf_op jit(solution)/shard_map/all_gather | solution.py:157
  246.9 38.8 %copy-start.45 = (bf16[128]{0:T(256)(128)(2,1)S(1)}, bf16[128]{0:T(256)(128)(2,1)}, u32[]{:S(2)}) copy-start(bf16[128]{0:T(256)(128)(2,1)} %param.29) | copy-start | bytes 772
  246.9 47.0 %copy-start.37 = (s32[384]{0:T(512)S(1)}, s32[384]{0:T(512)}, u32[]{:S(2)}) copy-start(s32[384]{0:T(512)} %param.21) | copy-start | bytes 4612
  255.2 38.7 %all-to-all-start.1 = ((bf16[4,384,256]{1,2,0:T(8,128)(2,1)}), bf16[4,384,256]{1,2,0:T(8,128)(2,1)}, u32[]{:S(2)}, u32[]{:S(2)}) async-start(bf16[4,384,256]{1,2,0:T(8,128)(2,1)} %copy.81), calls=%async_computation.1 | async-start | bytes 1572864 | tf_op jit(solution)/shard_map/all_to_all | solution.py:147
  259.9 361.8 %reduce-scatter.13.cloned.1.call-start = ((), (), s32[]{:S(2)}) async-start(), calls=%async_computation.18 | async-start | bytes 2359296 | tf_op jit(solution)/shard_map/reduce_scatter | solution.py:268
  293.9 68.3 %copy-start.25 = (f32[384]{0:T(512)}, f32[384]{0:T(512)S(1)}, u32[]{:S(2)}) copy-start(f32[384]{0:T(512)S(1)} %compare_convert_fusion) | copy-start | bytes 4612
  342.7 364.1 %reduce-scatter.17.cloned.1.call-start = ((), (), s32[]{:S(2)}) async-start(), calls=%async_computation.20 | async-start | bytes 9437184 | tf_op jit(solution)/shard_map/reduce_scatter | solution.py:280
  357.1 25.7 %all-to-all-start.2 = ((bf16[384,4,256]{2,0,1:T(8,128)(2,1)}), bf16[384,4,256]{2,0,1:T(8,128)(2,1)}, u32[]{:S(2)}, u32[]{:S(2)}) async-start(bf16[384,4,256]{2,0,1:T(8,128)(2,1)} %bitcast.123), calls=%async_computation.2 | async-start | bytes 1572864 | tf_op jit(solution)/shard_map/all_to_all | solution.py:191
  362.1 345.2 %reduce-scatter.21.cloned.1.call-start = ((), (), s32[]{:S(2)}) async-start(), calls=%async_computation.22 | async-start | bytes 9437184 | tf_op jit(solution)/shard_map/reduce_scatter | solution.py:286
  617.9 77.8 %all-to-all-start.3 = ((bf16[1536,3,256]{2,1,0:T(4,128)(2,1)}), bf16[1536,3,256]{2,1,0:T(4,128)(2,1)S(1)}, u32[]{:S(2)}, u32[]{:S(2)}) async-start(bf16[1536,3,256]{2,1,0:T(4,128)(2,1)} %copy.85), calls=%async_computation.3 | async-start | bytes 6291456 | tf_op jit(solution)/shard_map/all_to_all | solution.py:240
  621.6 107.6 %reduce-scatter.15.cloned.1.call-start = ((), (), s32[]{:S(2)}) async-start(), calls=%async_computation.19 | async-start | bytes 327680 | tf_op jit(solution)/shard_map/reduce_scatter | solution.py:309
  622.4 144.8 %reduce-scatter.9.cloned.1.call-start = ((), (), s32[]{:S(2)}) async-start(), calls=%async_computation.16 | async-start | bytes 7077888 | tf_op jit(solution)/shard_map/reduce_scatter | solution.py:259
  706.7 107.6 %reduce-scatter.19.cloned.1.call-start = ((), (), s32[]{:S(2)}) async-start(), calls=%async_computation.21 | async-start | bytes 1310720 | tf_op jit(solution)/shard_map/reduce_scatter | solution.py:321
  707.3 117.5 %reduce-scatter.23.cloned.1.call-start = ((), (), s32[]{:S(2)}) async-start(), calls=%async_computation.23 | async-start | bytes 1310720 | tf_op jit(solution)/shard_map/reduce_scatter | solution.py:327
  708.0 140.9 %reduce-scatter.11.cloned.1.call-start = ((), (), s32[]{:S(2)}) async-start(), calls=%async_computation.17 | async-start | bytes 983040 | tf_op jit(solution)/shard_map/reduce_scatter | solution.py:300
  738.3 32.8 %copy-start.40 = (bf16[1024]{0:T(1024)(128)(2,1)S(1)}, bf16[1024]{0:T(1024)(128)(2,1)}, u32[]{:S(2)}) copy-start(bf16[1024]{0:T(1024)(128)(2,1)} %get-tuple-element.165) | copy-start | bytes 6148
  738.3 72.8 %copy-start.10 = (f32[384,1024]{1,0:T(8,128)S(1)}, f32[384,1024]{1,0:T(8,128)}, u32[]{:S(2)}) copy-start(f32[384,1024]{1,0:T(8,128)} %copy-done.9) | copy-start | bytes 4718596
  738.3 72.7 %copy-start.16 = (bf16[384,1024]{1,0:T(8,128)(2,1)S(1)}, bf16[384,1024]{1,0:T(8,128)(2,1)}, u32[]{:S(2)}) copy-start(bf16[384,1024]{1,0:T(8,128)(2,1)} %param.35) | copy-start | bytes 2359300
  738.3 72.7 %copy-start.28 = (f32[384]{0:T(512)S(1)}, f32[384]{0:T(512)}, u32[]{:S(2)}) copy-start(f32[384]{0:T(512)} %copy-done.27) | copy-start | bytes 4612
  (52 other events, 612.5 us)
Sparse Core Ops, SparseCore 0:
  9.9 48.2 all-gather.14
  60.1 27.8 all-gather.16
  89.9 54.3 all-gather.18
  146.1 54.3 all-gather.20
  342.8 41.5 reduce-scatter.12
  388.1 71.2 reduce-scatter.16
  462.9 71.2 reduce-scatter.20
  624.8 27.2 reduce-scatter.14
  706.8 60.3 reduce-scatter.8
  769.4 27.1 reduce-scatter.18
  798.9 25.8 reduce-scatter.22
  827.1 21.8 reduce-scatter.10
where the time goes:
time: 865 us; the launch traced here: 858 us
  matrix products  265 us (31%)
  blocking collectives  190 us (22%)
  waiting for transfers between devices  160 us (18%)
  local copies, waits for them, and re-layouts  110 us (13%)
  other arithmetic  83.1 us (10%)
  starting transfers between devices  18.5 us (2%)
  between operations  17.6 us (2%)
  loops' own time  13.8 us (2%)
    all_gather x1, blocking collectives, shards(): span_labels = lax.all_gather(segment_ids, 'seq', axis=0, tiled=True)  75.7 us
    all_to_all x1, waiting for transfers between devices, shards(): lax.all_to_all(head_grads, 'seq', split_axis=0, concat_axis=2, tiled=True)  73.3 us
    dot_general x4, matrix products, block_scores(): jnp.einsum('qhd,khd->hqk', query_block, key_window, preferred_element_typ...  50.5 us
    dot_general x2, matrix products, block_backward(): jnp.einsum('qhd,khd->hqk', grad_block, value_window, preferred_element_ty...  44.4 us
    dynamic_update_slice x4, local copies, waits for them, and re-layouts, add_window(): return lax.dynamic_update_slice_in_dim(total, current + delta, start, 0)  39.2 us
    unnamed x2, blocking collectives  36.3 us
    convert_element_type x2, other arithmetic, block_backward(): grad_scores = (probs_full * (grad_probs - row_inner)).astype(jnp.bfloat16)  34.9 us
    dot_general x4, matrix products, contract_rows(): lax.dot_general(left, right, (((0,), (0,)), ((), ())), preferred_element_...  30.1 us
  transfers between devices with their start and end apart: 16, of which 6 were waited for; matrix products, arithmetic and copies ran while one was open for 49% of the time, Pallas kernels for 0%

commit v1 on v0

--- a/solution.py
+++ b/solution.py
@@ -3,6 +3,8 @@
 import jax
 import jax.numpy as jnp
 from jax import lax
+from jax.experimental import pallas as pl
+from jax.experimental.pallas import tpu as pltpu
 from jax.sharding import PartitionSpec as P
 
 HD = 64
@@ -48,7 +50,7 @@
     return lax.dynamic_update_slice_in_dim(total, current + delta, start, 0)
 
 
-def shards(
+def general_shards(
     tokens,
     segment_ids,
     ln1_gain,
@@ -348,6 +350,1021 @@
         summed[11],
         summed[12],
     )
+
+
+LX = (0, 4, 2, 6, 1, 5, 3, 7)
+LY = (0, 2, 4, 6, 1, 3, 5, 7)
+PAIR = ((0, 1), (1, 0), (2, 3), (3, 2))
+FAR = ((0, 2), (2, 0), (1, 3), (3, 1))
+CROSS = ((0, 3), (3, 0), (1, 2), (2, 1))
+BF = jnp.bfloat16
+F32 = jnp.float32
+RATE = 1e8
+SMEM_SPEC = pl.BlockSpec(memory_space=pltpu.SMEM)
+VMEM_SPEC = pl.BlockSpec(memory_space=pltpu.VMEM)
+HALF_ROOT = 0.7071067811865476
+DENSITY = 0.3989422804014327
+
+
+def fshift(values, bit, name="move"):
+    with jax.named_scope(name):
+        return lax.ppermute(values, "fsdp", [(i, i ^ bit) for i in range(8)])
+
+
+def zshift(values, pairs, name="move"):
+    with jax.named_scope(name):
+        return lax.ppermute(values, "seq", pairs)
+
+
+def after(values, *earlier):
+    return lax.optimization_barrier((values, *earlier))[0]
+
+
+def cost(micros):
+    return pl.CostEstimate(flops=int(micros * RATE) + 1, bytes_accessed=1, transcendentals=0)
+
+
+def call(body, outs, args, scratch=(), micros=1.0, limit=12, space=pltpu.VMEM):
+    single = not isinstance(outs, (list, tuple))
+    shapes = [outs] if single else list(outs)
+    result = pl.pallas_call(
+        body,
+        out_shape=shapes,
+        in_specs=[SMEM_SPEC] + [pl.BlockSpec(memory_space=space)] * (len(args) - 1),
+        out_specs=[VMEM_SPEC] * len(shapes),
+        scratch_shapes=list(scratch),
+        compiler_params=pltpu.CompilerParams(vmem_limit_bytes=limit * 2**20),
+        cost_estimate=cost(micros),
+    )(*args)
+    return result[0] if single else result
+
+
+def struct(shape, dtype):
+    return jax.ShapeDtypeStruct(shape, dtype)
+
+
+def lanes_low(shape):
+    return lax.broadcasted_iota(jnp.int32, shape, 1) < HD
+
+
+def dot_nn(a, b):
+    return lax.dot_general(a, b, (((1,), (0,)), ((), ())), preferred_element_type=F32)
+
+
+def dot_nt(a, b):
+    return lax.dot_general(a, b, (((1,), (1,)), ((), ())), preferred_element_type=F32)
+
+
+def dot_tn(a, b):
+    return lax.dot_general(a, b, (((0,), (0,)), ((), ())), preferred_element_type=F32)
+
+
+def offset(index, size):
+    return pl.multiple_of(index * size, size)
+
+
+def natural(ref, start):
+    return jnp.concatenate([ref[i : i + 1, start : start + 128] for i in range(8)], axis=1)
+
+
+def pick_qkv(ids, w_hbm, tokens_hbm, *refs):
+    count = (len(refs) - 4) // 2
+    rows_hbm, (out_ref, extra_ref, w_ref), rows, sems = refs[:count], refs[count : count + 3], refs[count + 3 : -1], refs[-1]
+    cut = tokens_hbm.shape[0] // 2
+    copies = [(w_hbm, w_ref), (tokens_hbm.at[pl.ds(cut, cut)], extra_ref), *zip(rows_hbm, rows)]
+    copies = [pltpu.make_async_copy(source, target, sems.at[i]) for i, (source, target) in enumerate(copies)]
+    for copy in copies:
+        copy.start()
+    for copy in copies:
+        copy.wait()
+    half = ids[1] % 2
+    low = lanes_low((128, 128))
+    for j in range(w_ref.shape[1] // 256):
+        first = w_ref[:, 256 * j : 256 * j + 128].astype(F32)
+        second = w_ref[:, 256 * j + 128 : 256 * j + 256].astype(F32)
+        even = jnp.where(low, first, pltpu.roll(second, HD, 1))
+        odd = jnp.where(low, pltpu.roll(first, HD, 1), second)
+        out_ref[0:128, 128 * j : 128 * j + 128] = jnp.where(half == 0, even, odd).astype(BF)
+    start = 0
+    for row_ref in rows:
+        size = row_ref.shape[0]
+        row = row_ref[...].astype(F32)
+        out_ref[128:144, start : start + size] = jnp.broadcast_to(row.reshape(1, size), (16, size)).astype(BF)
+        start += size
+
+
+def pick_mlp(ids, w1_hbm, w2_hbm, wo_hbm, one_ref, two_ref, out_ref, sems):
+    half = ids[1] % 2
+    out_hbm = wo_hbm.at[pl.ds(offset(half, 64), 64)]
+    copies = [
+        (w2_hbm.at[pl.ds(offset(half, 256), 256)], two_ref.at[pl.ds(0, 256)]),
+        (out_hbm, out_ref),
+        (out_hbm, one_ref.at[pl.ds(256, 64)]),
+        (out_hbm, two_ref.at[pl.ds(256, 64)]),
+    ]
+    for b in range(8):
+        rows, lanes = pl.ds(128 * (b // 4), 128), pl.ds(256 * (b % 4), 256)
+        copies.append((w1_hbm.at[:, pl.ds(offset(2 * b + half, 256), 256)], one_ref.at[rows, lanes]))
+    copies = [pltpu.make_async_copy(source, target, sems.at[i]) for i, (source, target) in enumerate(copies)]
+    for copy in copies:
+        copy.start()
+    for copy in copies:
+        copy.wait()
+
+
+def stack_mlp_body(ids, one_ref, one_x_ref, two_ref, two_y_ref, out_ref, one_out, two_out, outs):
+    one_out[0:256, :] = one_ref[0:256, :]
+    one_out[256:512, :] = one_x_ref[0:256, :]
+    two_out[0:256, :] = two_ref[0:256, :]
+    two_out[256:512, :] = two_y_ref[0:256, :]
+    outs[0:64, :] = one_ref[256:320, :]
+    outs[64:128, :] = one_x_ref[256:320, :]
+    outs[128:192, :] = two_y_ref[256:320, :]
+    outs[192:256, :] = out_ref[...]
+
+
+def stack_body(ids, *refs):
+    out_ref = refs[-1]
+    start = 0
+    for ref in refs[:-1]:
+        out_ref[start : start + ref.shape[0], :] = ref[...]
+        start += ref.shape[0]
+
+
+def stack(ids, *arrays):
+    rows = sum(a.shape[0] for a in arrays)
+    return call(stack_body, struct((rows, arrays[0].shape[1]), BF), (ids, *arrays), micros=0.7)
+
+
+def place_rows(ids, own_ref, theirs_ref, two_ref, three_ref, out_ref):
+    half = ids[1] % 2
+    pair = ids[1] // 2
+    own_rows = own_ref.shape[0]
+    cut = two_ref.shape[0]
+    tail = out_ref.shape[0] - own_rows - cut
+    for value in range(2):
+        first, second = (own_ref, theirs_ref) if value == 0 else (theirs_ref, own_ref)
+
+        @pl.when(half == value)
+        def _():
+            out_ref[0:own_rows, :] = first[...]
+
+        @pl.when((half == value) & (pair == 0))
+        def _():
+            out_ref[own_rows:, :] = second[0 : cut + tail, :]
+
+        @pl.when((half == value) & (pair == 1))
+        def _():
+            out_ref[own_rows + cut :, :] = second[0:tail, :]
+
+    @pl.when(pair == 1)
+    def _():
+        out_ref[own_rows : own_rows + cut, :] = two_ref[...] + three_ref[...]
+
+
+def place_grad_body(ids, own_ref, theirs_ref, two_ref, three_ref, out_ref):
+    place_rows(ids, own_ref, theirs_ref, two_ref, three_ref, out_ref)
+    own_rows = own_ref.shape[0]
+    rows = out_ref.shape[0]
+    live = key_valid(ids, (rows - own_rows, 1), 0, own_rows, own_rows)
+    tail = out_ref[own_rows:, :].astype(F32)
+    out_ref[own_rows:, :] = jnp.where(live, tail, 0.0).astype(BF)
+
+
+def parts_of(refs):
+    a, x, y, d, other = refs
+    parts = {0: (a, 0), 2: (x, 0), 4: (y, 0), 6: (d, 0)}
+    parts.update({2 * i + 1: (other, 144 * i) for i in range(4)})
+    return parts
+
+
+def piece_tile(parts, k, lanes):
+    ref, row = parts[k]
+    return ref[row : row + 128, lanes]
+
+
+def qkv_body(ids, own_ref, theirs_ref, two_ref, three_ref, *refs):
+    parts = parts_of(refs[:5])
+    x_ref, qkv_ref, even_ref, odd_ref, par_ref, norm_ref, bias_ref = refs[5:]
+    place_rows(ids, own_ref, theirs_ref, two_ref, three_ref, x_ref)
+    f = ids[0]
+    half = ids[1] % 2
+    rows = x_ref.shape[0]
+    for k in range(8):
+        ref, at = parts[k]
+        par_ref[pl.ds(f ^ k, 1), :] = ref[at + 128 : at + 129, :].astype(F32)
+    gain = natural(par_ref, 0)
+    shift = natural(par_ref, 128)
+    low = lanes_low((1, 128))
+    bias_ref[...] = jnp.zeros_like(bias_ref)
+    for start, place in ((768, 0), (896, 1024)):
+        block = par_ref[:, start : start + 128]
+        turned = pltpu.roll(block, HD, 1)
+        lower = jnp.where(half == 0, block, turned)
+        upper = jnp.where(half == 0, turned, block)
+        for j in range(4):
+            bias_ref[:, place + 128 * j : place + 128 * j + 128] = jnp.where(
+                low, lower[2 * j : 2 * j + 1], upper[2 * j + 1 : 2 * j + 2]
+            )
+
+    def norm(i, carry):
+        at = pl.ds(offset(i, 32), 32)
+        values = x_ref[at, :].astype(F32)
+        norm_ref[at, :] = normalize(values, gain, shift).astype(BF)
+        return carry
+
+    lax.fori_loop(0, rows // 32, norm, 0)
+    for place, k in enumerate(LY):
+        target = even_ref if place < 4 else odd_ref
+        column = 128 * (place % 4)
+        target[:, column : column + 128] = norm_ref[:, pl.ds(offset(f ^ k, 128), 128)]
+    left = jnp.concatenate([even_ref[...], odd_ref[...]], axis=1)
+    for n in range(6):
+        lanes = slice(256 * n, 256 * n + 256)
+        weight = jnp.concatenate([piece_tile(parts, k, lanes) for k in LY], axis=0)
+        qkv_ref[:, lanes] = (dot_nn(left, weight) + bias_ref[:, lanes]).astype(BF)
+
+
+def key_valid(ids, shape, axis, own_rows, first=0):
+    pair = ids[1] // 2
+    place = lax.broadcasted_iota(jnp.int32, shape, axis) + first
+    return (place < LEN + pair) & ((place != own_rows) | (pair == 0))
+
+
+def head_masked(block, head, factor=None):
+    wide = block.astype(F32)
+    low = lanes_low(wide.shape)
+    keep = low if head == 0 else jnp.logical_not(low)
+    if factor is not None:
+        wide = wide * factor
+    return jnp.where(keep, wide, 0.0).astype(BF)
+
+
+def attend_body(own_rows, tile, ids, q_ref, k_ref, v_ref, o_ref):
+    rows = q_ref.shape[0]
+    value = v_ref[...]
+    live = key_valid(ids, (1, rows), 1, own_rows)
+    low = lanes_low((tile, 128))
+    keys = [head_masked(k_ref[...], head, HD**-0.5) for head in range(2)]
+    for t in range(rows // tile):
+        at = slice(t * tile, t * tile + tile)
+        outs = []
+        for head in range(2):
+            scores = jnp.where(live, dot_nt(q_ref[at, :], keys[head]), masked_score)
+            peak = jnp.max(scores, axis=1, keepdims=True)
+            lifted = jnp.exp(scores - peak)
+            total = jnp.sum(lifted, axis=1, keepdims=True)
+            outs.append(dot_nn(lifted.astype(BF), value) / total)
+        o_ref[at, :] = jnp.where(low, outs[0], outs[1]).astype(BF)
+
+
+def attend_back_body(own_rows, tile, ids, q_ref, k_ref, v_ref, g0_ref, g1_ref, gq_ref, gk_ref, gv_ref):
+    rows = q_ref.shape[0]
+    whole = jnp.concatenate([g0_ref[...], g1_ref[...]], axis=0)
+    scale = HD**-0.5
+    live = key_valid(ids, (rows, 1), 0, own_rows)
+    low = lanes_low((rows, 128))
+    grads_k = []
+    grads_v = []
+    for t in range(rows // tile):
+        at = slice(t * tile, t * tile + tile)
+        query = q_ref[at, :]
+        grad = whole[at]
+        grad_q = None
+        for head in range(2):
+            keys = head_masked(k_ref[...], head, scale)
+            values = head_masked(v_ref[...], head)
+            scores = jnp.where(live, dot_nt(keys, query), masked_score)
+            peak = jnp.max(scores, axis=0, keepdims=True)
+            lifted = jnp.exp(scores - peak)
+            probs = lifted * (1.0 / jnp.sum(lifted, axis=0, keepdims=True))
+            grad_p = dot_nt(values, grad)
+            inner = jnp.sum(grad_p * probs, axis=0, keepdims=True)
+            grad_s = (probs * (grad_p - inner)).astype(BF)
+            grad_v = dot_nn(probs.astype(BF), grad)
+            grad_k = dot_nn(grad_s, query) * scale
+            part = dot_tn(grad_s, keys)
+            grad_q = part if grad_q is None else grad_q + part
+            if t == 0:
+                grads_k.append(grad_k)
+                grads_v.append(grad_v)
+            else:
+                grads_k[head] = grads_k[head] + grad_k
+                grads_v[head] = grads_v[head] + grad_v
+        gq_ref[at, :] = grad_q.astype(BF)
+    gk_ref[...] = jnp.where(low, grads_k[0], grads_k[1]).astype(BF)
+    gv_ref[...] = jnp.where(low, grads_v[0], grads_v[1]).astype(BF)
+
+
+def mixed_body(ids, o_ref, even_ref, odd_ref, first_ref, second_ref, w_ref):
+    f = ids[0]
+    for place, k in enumerate((0, 2, 4, 6)):
+        row = HD * place
+        w_ref[pl.ds(offset(f ^ k, HD), HD), :] = even_ref[row : row + HD, :]
+        w_ref[pl.ds(offset(f ^ k ^ 1, HD), HD), :] = odd_ref[row : row + HD, :]
+    size = first_ref.shape[0]
+    for n in range(4):
+        lanes = slice(256 * n, 256 * n + 256)
+        first_ref[:, lanes] = dot_nn(o_ref[0:size, :], w_ref[:, lanes]).astype(BF)
+    for n in range(4):
+        lanes = slice(256 * n, 256 * n + 256)
+        second_ref[:, lanes] = dot_nn(o_ref[size:, :], w_ref[:, lanes]).astype(BF)
+
+
+def mlp_body(base, ids, par_ref, x_ref, mine_ref, theirs_ref, gm_ref, one_a, one_b, two_a, two_b, *refs):
+    (mid_ref, even_ref, odd_ref, act_e_ref, act_o_ref, gu_ref, gh_ref, bias_ref, norm_ref, u_ref, g_ref) = refs
+    f = ids[0]
+    half = ids[1] % 2
+    rows = mid_ref.shape[0]
+    gain = natural(par_ref, 384)
+    shift = natural(par_ref, 512)
+    bias = natural(par_ref, 256)
+
+    def one_rows(place, start, size, lanes):
+        ref = one_a if place < 4 else one_b
+        return ref[pl.ds(256 * (place % 4) + start, size), lanes]
+
+    def norm(i, carry):
+        at = pl.ds(offset(i, 32), 32)
+        middle = x_ref[pl.ds(pl.multiple_of(base + i * 32, 32), 32), :].astype(F32)
+        middle = middle + (mine_ref[at, :].astype(F32) + theirs_ref[at, :].astype(F32) + bias)
+        mid_ref[at, :] = middle
+        norm_ref[at, :] = normalize(middle, gain, shift).astype(BF)
+        return carry
+
+    lax.fori_loop(0, rows // 32, norm, 0)
+    for place, k in enumerate(LY):
+        target = even_ref if place < 4 else odd_ref
+        column = 128 * (place % 4)
+        target[:, column : column + 128] = norm_ref[:, pl.ds(offset(f ^ k, 128), 128)]
+    left = jnp.concatenate([even_ref[...], odd_ref[...]], axis=1)
+    grad = gm_ref[base : base + rows, :]
+    for place, k in enumerate(LX):
+        block = f ^ k
+        at_lanes = pl.ds(offset(block % 4, 256), 256)
+        weight = jnp.concatenate([one_rows(j, offset(block // 4, 128), 128, at_lanes) for j in range(8)], axis=0)
+        u_ref[...] = dot_nn(left, weight)
+        two_ref = two_a if place < 4 else two_b
+        g_ref[...] = dot_nt(grad, two_ref[256 * (place % 4) : 256 * (place % 4) + 256, :])
+        row = par_ref[pl.ds(block, 1), pl.ds(offset(4 + half, 256), 256)]
+        act_ref = act_e_ref if place < 4 else act_o_ref
+        column = 256 * (place % 4)
+
+        def gelu(i, total):
+            at = pl.ds(offset(i, 32), 32)
+            u = u_ref[at, :] + row
+            cdf = 0.5 + 0.5 * lax.erf(u * HALF_ROOT)
+            act_ref[at, column : column + 256] = (u * cdf).astype(BF)
+            slope = cdf + u * (jnp.exp(-0.5 * (u * u)) * DENSITY)
+            gu = (g_ref[at, :] * slope).astype(BF)
+            gu_ref[at, pl.ds(offset(block, 256), 256)] = gu
+            return total + jnp.sum(gu.astype(F32), axis=0, keepdims=True)
+
+        total = lax.fori_loop(0, rows // 32, gelu, jnp.zeros((1, 256), F32))
+        bias_ref[pl.ds(block, 1), :] = total
+    for j in range(4):
+        total = None
+        for part in range(2):
+            weight = jnp.concatenate(
+                [one_rows(place, 128 * part, 128, slice(None)) for place in (2 * j, 2 * j + 1)], axis=0
+            )
+            term = dot_nt(gu_ref[:, 1024 * part : 1024 * part + 1024], weight)
+            total = term if total is None else total + term
+        gh_ref[:, pl.ds(offset(f ^ LY[2 * j], 128), 128)] = total[:, 0:128].astype(BF)
+        gh_ref[:, pl.ds(offset(f ^ LY[2 * j + 1], 128), 128)] = total[:, 128:256].astype(BF)
+
+
+def out_body(ids, e0_ref, o0_ref, e1_ref, o1_ref, two_a, two_b, keep_ref, send_ref, y_ref):
+    half = ids[1] % 2
+    for n in range(4):
+        lanes = slice(256 * n, 256 * n + 256)
+        weight = jnp.concatenate([two_a[:, lanes], two_b[:, lanes]], axis=0)
+        start = 0
+        for e_ref, o_ref in ((e0_ref, o0_ref), (e1_ref, o1_ref)):
+            left = jnp.concatenate([e_ref[...], o_ref[...]], axis=1)
+            y_ref[start : start + left.shape[0], lanes] = dot_nn(left, weight).astype(BF)
+            start += left.shape[0]
+    rows = keep_ref.shape[0]
+    shift = y_ref.shape[0] - rows
+    keep_ref[...] = y_ref[pl.ds(offset(half, shift), rows), :]
+    send_ref[...] = y_ref[pl.ds(offset(1 - half, shift), rows), :]
+
+
+def result_body(ids, par_ref, mid0_ref, mid1_ref, mine_ref, theirs_ref, out_ref, extra_ref):
+    half = ids[1] % 2
+    bias = natural(par_ref, 640)
+    rows = out_ref.shape[0]
+    shift = mid0_ref.shape[0] + mid1_ref.shape[0] - rows
+
+    def step(i, carry):
+        at = pl.ds(offset(i, 32), 32)
+        place = half * shift + i * 32
+        total = mine_ref[at, :].astype(F32) + theirs_ref[at, :].astype(F32) + bias
+        size = mid0_ref.shape[0]
+
+        @pl.when(place < size)
+        def _():
+            out_ref[at, :] = (total + mid0_ref[pl.ds(pl.multiple_of(place, 32), 32), :]).astype(BF)
+
+        @pl.when(place >= size)
+        def _():
+            out_ref[at, :] = (total + mid1_ref[pl.ds(pl.multiple_of(place - size, 32), 32), :]).astype(BF)
+
+        return carry
+
+    lax.fori_loop(0, rows // 32, step, 0)
+    spot = rows - shift
+    extra_ref[...] = out_ref[spot : spot + extra_ref.shape[0], :]
+
+
+def owner_rows_body(ids, valid_ref, full_ref, extra_ref, out_ref):
+    half = ids[1] % 2
+    pair = ids[1] // 2
+    rows, cut = full_ref.shape[0], extra_ref.shape[0]
+    tail = 2 * cut + 32 - rows
+    shift = cut + tail
+    spot = rows - shift
+    width = full_ref.shape[1]
+
+    def masked(at, values):
+        valid = jnp.concatenate([valid_ref[at, :]] * (width // 128), axis=1)
+        return jnp.where(valid > 0.0, values.astype(F32), 0.0).astype(out_ref.dtype)
+
+    @pl.when(half == 0)
+    def _():
+        out_ref[...] = masked(slice(None), full_ref[...])
+
+    @pl.when((half == 1) & (pair == 0))
+    def _():
+        top = slice(0, cut)
+        out_ref[top, :] = masked(top, full_ref[spot : spot + cut, :])
+        low = slice(cut, rows)
+        border = full_ref[spot + cut : spot + cut + 1, :].astype(F32)
+        first = lax.broadcasted_iota(jnp.int32, (cut, 1), 0) == 0
+        out_ref[low, :] = masked(low, jnp.where(first, border, extra_ref[...].astype(F32)))
+
+    @pl.when((half == 1) & (pair == 1))
+    def _():
+        top = slice(0, tail)
+        out_ref[top, :] = masked(top, full_ref[spot + cut : spot + cut + tail, :])
+        out_ref[tail:rows, :] = jnp.zeros((rows - tail, width), out_ref.dtype)
+
+
+def rows_grad_body(step, ids, l0_ref, l1_ref, r0_ref, r1_ref, out_ref):
+    rows = l0_ref.shape[0] + l1_ref.shape[0]
+    left = jnp.concatenate([l0_ref[...], l1_ref[...]], axis=0)
+    for n in range(out_ref.shape[1] // step):
+        lanes = slice(step * n, step * n + step)
+        if r0_ref.shape[0] == rows:
+            right = r0_ref[:, lanes]
+        else:
+            right = jnp.concatenate([r0_ref[:, lanes], r1_ref[:, lanes]], axis=0)
+        out_ref[:, lanes] = dot_tn(left, right).astype(BF)
+
+
+def norm_back(values, grad, gain):
+    center = values - jnp.mean(values, axis=-1, keepdims=True)
+    scale = lax.rsqrt(jnp.mean(center * center, axis=-1, keepdims=True) + norm_eps)
+    unit = center * scale
+    scaled = grad * gain
+    first = jnp.mean(scaled, axis=-1, keepdims=True)
+    second = jnp.mean(scaled * unit, axis=-1, keepdims=True)
+    return unit, scale * (scaled - first - unit * second)
+
+
+def fold(values):
+    total = values[0:8]
+    for i in range(1, values.shape[0] // 8):
+        total = total + values[8 * i : 8 * i + 8]
+    return total
+
+
+def spread(ref, start, partial_rows):
+    row = jnp.sum(partial_rows, axis=0, keepdims=True)
+    for i in range(8):
+        ref[i : i + 1, start : start + 128] = row[:, 128 * i : 128 * i + 128]
+
+
+def middle_back_body(base, ids, par_ref, mid_ref, gm_ref, mine_ref, theirs_ref, w_ref, gb_ref, go_ref, sums_ref):
+    half = ids[1] % 2
+    counts = jnp.where(half == 0, 1.0, 0.0)
+    gain = natural(par_ref, 384)
+    rows = mid_ref.shape[0]
+
+    def step(i, carry):
+        out_sum, gain_sum, shift_sum, last_sum = carry
+        at = pl.ds(offset(i, 32), 32)
+        mine = mine_ref[at, :].astype(F32)
+        grad = mine + theirs_ref[at, :].astype(F32)
+        unit, back = norm_back(mid_ref[at, :], grad, gain)
+        gm = gm_ref[pl.ds(pl.multiple_of(base + i * 32, 32), 32), :].astype(F32)
+        gb = (gm + back).astype(BF)
+        gb_ref[at, :] = gb
+        return (
+            out_sum + fold(gb.astype(F32)),
+            gain_sum + fold(mine * unit),
+            shift_sum + fold(mine),
+            last_sum + fold(gm),
+        )
+
+    zero = jnp.zeros((8, mid_ref.shape[1]), F32)
+    sums = lax.fori_loop(0, rows // 32, step, (zero, zero, zero, zero))
+    spread(sums_ref, 0, sums[0] * counts)
+    spread(sums_ref, 128, sums[1])
+    spread(sums_ref, 256, sums[2])
+    spread(sums_ref, 384, sums[3] * counts)
+    grad = gb_ref[...]
+    for n in range(2):
+        rows = slice(256 * n, 256 * n + 256)
+        go_ref[:, rows] = dot_nt(grad, w_ref[rows, :]).astype(BF)
+
+
+def out_grad_body(ids, o_ref, gb0_ref, gb1_ref, keep_ref, send_ref, grad_ref):
+    f = ids[0]
+    for n in range(4):
+        lanes = slice(256 * n, 256 * n + 256)
+        right = jnp.concatenate([gb0_ref[:, lanes], gb1_ref[:, lanes]], axis=0)
+        grad_ref[:, lanes] = dot_tn(o_ref[...], right).astype(BF)
+    for place, k in enumerate(LX):
+        target = keep_ref if place < 4 else send_ref
+        row = HD * (place % 4)
+        target[row : row + HD, :] = grad_ref[pl.ds(offset(f ^ k, HD), HD), :]
+
+
+def input_grad_body(ids, x_ref, par_ref, gq_ref, gk_ref, gv_ref, *refs):
+    parts = parts_of(refs[:5])
+    keep_ref, send_ref, sums_ref, wide_ref, gh_ref = refs[5:]
+    f = ids[0]
+    left = jnp.concatenate([gq_ref[...], gk_ref[...], gv_ref[...]], axis=1)
+    for j in range(4):
+        first, second = LY[2 * j], LY[2 * j + 1]
+        weight = jnp.concatenate(
+            [piece_tile(parts, first, slice(None)), piece_tile(parts, second, slice(None))], axis=0
+        )
+        total = dot_nt(left, weight)
+        wide_ref[:, pl.ds(offset(f ^ first, 128), 128)] = total[:, 0:128]
+        wide_ref[:, pl.ds(offset(f ^ second, 128), 128)] = total[:, 128:256]
+
+    def step(i, carry):
+        gain_sum, shift_sum = carry
+        at = pl.ds(offset(i, 32), 32)
+        grad = wide_ref[at, :]
+        gh_ref[at, :] = grad.astype(BF)
+        values = x_ref[at, :].astype(F32)
+        center = values - jnp.mean(values, axis=-1, keepdims=True)
+        unit = center * lax.rsqrt(jnp.mean(center * center, axis=-1, keepdims=True) + norm_eps)
+        return gain_sum + fold(grad * unit), shift_sum + fold(grad)
+
+    zero = jnp.zeros((8, x_ref.shape[1]), F32)
+    gain_sum, shift_sum = lax.fori_loop(0, x_ref.shape[0] // 32, step, (zero, zero))
+    half = ids[1] % 2
+    rows = keep_ref.shape[0]
+    shift = x_ref.shape[0] - rows
+    keep_ref[...] = gh_ref[pl.ds(offset(half, shift), rows), :]
+    send_ref[...] = gh_ref[pl.ds(offset(1 - half, shift), rows), :]
+    spread(sums_ref, 0, gain_sum)
+    spread(sums_ref, 128, shift_sum)
+
+
+def qkv_grad_body(ids, even_ref, odd_ref, gq_ref, gk_ref, gv_ref, one_ref, mid0_ref, mid1_ref, fc0_ref, fc1_ref, *refs):
+    keep_ref, send_ref, par_ref = refs
+    f = ids[0]
+    half = ids[1] % 2
+    par_ref[:, 0:256] = one_ref[...]
+    par_ref[:, 256:768] = mid0_ref[...] + mid1_ref[...]
+    fc_sum = fc0_ref[...] + fc1_ref[...]
+    low = lanes_low((1, 128))
+    mine = low == (half == 0)
+    for g_ref, place in ((gq_ref, 768), (gv_ref, 896)):
+        row = jnp.sum(g_ref[...].astype(F32), axis=0, keepdims=True)
+        for j in range(4):
+            block = row[:, 128 * j : 128 * j + 128]
+            turned = pltpu.roll(jnp.broadcast_to(block, (8, 128)), HD, 1)[0:1]
+            first = jnp.where(half == 0, block, turned)
+            second = jnp.where(half == 0, turned, block)
+            par_ref[2 * j : 2 * j + 1, place : place + 128] = jnp.where(mine, first, 0.0)
+            par_ref[2 * j + 1 : 2 * j + 2, place : place + 128] = jnp.where(mine, second, 0.0)
+    zero = jnp.zeros((8, 256), F32)
+    par_ref[:, 1024:1280] = jnp.where(half == 0, fc_sum, zero)
+    par_ref[:, 1280:1536] = jnp.where(half == 1, fc_sum, zero)
+    order_b = LY
+    place_a = {k: i for i, k in enumerate(LX)}
+    for j in range(4):
+        source = even_ref if j < 2 else odd_ref
+        left = source[:, 256 * (j % 2) : 256 * (j % 2) + 256]
+        for n, g_ref in enumerate((gq_ref, gk_ref, gv_ref)):
+            lanes = slice(512 * n, 512 * n + 512)
+            total = dot_tn(left, g_ref[...]).astype(BF)
+            for i in range(2):
+                k = order_b[2 * j + i]
+                target = keep_ref if place_a[k] < 4 else send_ref
+                row = 64 * (place_a[k] % 4)
+                target[row : row + 64, lanes] = total[128 * i : 128 * i + 64]
+                row = 256 + 80 * ((2 * j + i) % 4)
+                target[row : row + 64, lanes] = total[128 * i + 64 : 128 * i + 128]
+    for place, k in enumerate(order_b):
+        target = keep_ref if place < 4 else send_ref
+        row = 320 + 80 * (place % 4)
+        target[row : row + 16, :] = jnp.broadcast_to(par_ref[pl.ds(f ^ k, 1), :], (16, 1536)).astype(BF)
+
+
+def input_back_body(ids, par_ref, x_ref, gb0_ref, gb1_ref, mine_ref, theirs_ref, out_ref, extra_ref, gb_ref):
+    half = ids[1] % 2
+    gain = natural(par_ref, 0)
+    rows = out_ref.shape[0]
+    shift = x_ref.shape[0] - rows
+    size = gb0_ref.shape[0]
+    gb_ref[0:size, :] = gb0_ref[...]
+    gb_ref[size:, :] = gb1_ref[...]
+
+    def step(i, carry):
+        at = pl.ds(offset(i, 32), 32)
+        place = pl.ds(pl.multiple_of(half * shift + i * 32, 32), 32)
+        grad = mine_ref[at, :].astype(F32) + theirs_ref[at, :].astype(F32)
+        back = norm_back(x_ref[place, :].astype(F32), grad, gain)[1]
+        out_ref[at, :] = gb_ref[place, :].astype(F32) + back
+        return carry
+
+    lax.fori_loop(0, rows // 32, step, 0)
+    spot = rows - shift
+    extra_ref[...] = out_ref[spot : spot + extra_ref.shape[0], :].astype(BF)
+
+
+def line_body(ids, ka_ref, ra_ref, kb_ref, rb_ref, *outs):
+    s = ids[1]
+    wide_a, wide_b = outs[4:]
+    wide_a[...] = halve(ka_ref[...], ra_ref[...])
+    wide_b[...] = halve(kb_ref[...], rb_ref[...])
+    for turn in range(4):
+        lanes = pl.ds(offset(s ^ turn, 384), 384)
+        out_ref = outs[turn]
+        out_ref[0:64, :] = wide_a[:, lanes]
+        out_ref[64:128, :] = wide_b[0:64, lanes]
+        for i in range(4):
+            out_ref[128 + 16 * i : 144 + 16 * i, :] = wide_b[64:80, 384 * i : 384 * i + 384]
+
+
+def line_mlp_body(ids, k2_ref, r2_ref, k1_ref, r1_ref, *outs):
+    s = ids[1]
+    two, one = outs[4:]
+    two[...] = halve(k2_ref[...], r2_ref[...])
+    one[...] = halve(k1_ref[...], r1_ref[...])
+    for turn in range(4):
+        t = s ^ turn
+        out_ref = outs[turn]
+        out_ref[0:256, :] = two[0:256, pl.ds(offset(t, 256), 256)]
+        for i in range(2):
+            out_ref[256 + 128 * i : 384 + 128 * i, :] = one[:, pl.ds(offset(2 * t + i, 256), 256)]
+        out_ref[512:576, :] = two[256:320, pl.ds(offset(t, 256), 256)]
+
+
+def merge_body(plan, ids, *refs):
+    count = sum(len(group) for group in plan)
+    at = 0
+    for place, group in enumerate(plan):
+        stay_ref, send_ref = refs[2 * count + 2 * place : 2 * count + 2 * place + 2]
+        row = 0
+        for start, rows in group:
+            keep_ref, got_ref = refs[2 * at : 2 * at + 2]
+            half = rows // 2
+            stay_ref[row : row + half, :] = halve(keep_ref[start : start + half, :], got_ref[start : start + half, :])
+            send_ref[row : row + half, :] = halve(
+                keep_ref[start + half : start + rows, :], got_ref[start + half : start + rows, :]
+            )
+            row += half
+            at += 1
+
+
+def merge(ids, *groups):
+    plan = tuple(tuple((start, rows) for _, _, start, rows in group) for group in groups)
+    shapes = []
+    for group in groups:
+        rows = sum(g[3] for g in group) // 2
+        shapes += [struct((rows, group[0][0].shape[1]), BF)] * 2
+    operands = [a for group in groups for g in group for a in g[:2]]
+    return call(partial(merge_body, plan), shapes, (ids, *operands), micros=1.0)
+
+
+def join_mlp_body(ids, own_ref, pair_ref, far_ref, cross_ref, one_ref, two_ref, out_ref):
+    half = ids[1] % 2
+    other = 1 - half
+
+    def sums(at):
+        same = own_ref[at, :].astype(F32) + far_ref[at, :].astype(F32)
+        return same, pair_ref[at, :].astype(F32) + cross_ref[at, :].astype(F32)
+
+    same, rest = sums(slice(0, 256))
+    two_ref[pl.ds(offset(half, 256), 256), :] = same
+    two_ref[pl.ds(offset(other, 256), 256), :] = rest
+    for i in range(2):
+        same, rest = sums(slice(256 + 128 * i, 384 + 128 * i))
+        one_ref[:, pl.ds(offset(2 * i + half, 256), 256)] = same
+        one_ref[:, pl.ds(offset(2 * i + other, 256), 256)] = rest
+    same, rest = sums(slice(512, 576))
+    out_ref[pl.ds(offset(half, 64), 64), :] = same
+    out_ref[pl.ds(offset(other, 64), 64), :] = rest
+
+
+def join_body(ids, own_ref, pair_ref, far_ref, cross_ref, out_ref, sums_ref, wide_ref):
+    s = ids[1]
+    lower = s % 2 == 0
+    low = lanes_low((128, 128))
+    for j in range(3):
+        lanes = slice(128 * j, 128 * j + 128)
+        same = own_ref[0:128, lanes].astype(F32) + far_ref[0:128, lanes].astype(F32)
+        other = pair_ref[0:128, lanes].astype(F32) + cross_ref[0:128, lanes].astype(F32)
+        first = jnp.where(lower, same, other)
+        second = jnp.where(lower, other, same)
+        out_ref[:, 256 * j : 256 * j + 128] = jnp.where(low, first, pltpu.roll(second, HD, 1))
+        out_ref[:, 256 * j + 128 : 256 * j + 256] = jnp.where(low, pltpu.roll(first, HD, 1), second)
+    for i in range(4):
+        at = slice(128 + 16 * i, 144 + 16 * i)
+        total = own_ref[at, :].astype(F32) + far_ref[at, :].astype(F32)
+        total = total + pair_ref[at, :].astype(F32) + cross_ref[at, :].astype(F32)
+        for n in range(3):
+            spot = 3 * i + n
+            block = total[0:8, 128 * n : 128 * n + 128]
+            if spot < 8:
+                sums_ref[spot : spot + 1, :] = pltpu.roll(block, (128 - 32 * s) % 128, 1)[0:1]
+            else:
+                wide_ref[spot - 8 : spot - 7, :] = block[0:1]
+    sums_ref[8:9, :] = wide_ref[pl.ds(s, 1), :]
+
+
+def halve(keep, received):
+    return (keep.astype(F32) + received.astype(F32)).astype(BF)
+
+
+def paired_shards(
+    tokens,
+    segment_ids,
+    ln1_gain,
+    ln1_bias,
+    w_qkv,
+    q_bias,
+    v_bias,
+    w_out,
+    out_bias,
+    ln2_gain,
+    ln2_bias,
+    w_fc1,
+    fc1_bias,
+    w_fc2,
+    fc2_bias,
+    cotangent,
+):
+    own_rows, width = tokens.shape
+    cut = own_rows // 2
+    tail = 32
+    rows = own_rows + cut + tail
+    f = lax.axis_index("fsdp")
+    s = lax.axis_index("seq")
+    ids = jnp.where(lax.iota(jnp.int32, 2) == 0, f, s).astype(jnp.int32)
+
+    def exchange(own, extra, name):
+        extra = zshift(extra, ((1, 2),), name + "_extra")
+        return zshift(own, PAIR, name), extra, zshift(extra, ((2, 3),), name + "_relay")
+
+    hbm = partial(pltpu.with_memory_space_constraint, memory_space=pltpu.HBM)
+    vectors = [ln1_gain, ln1_bias, out_bias, ln2_gain, ln2_bias, fc2_bias, q_bias, v_bias, fc1_bias]
+    a, tokens_extra = call(
+        pick_qkv,
+        [struct((144, 1536), BF), struct((own_rows - cut, width), BF)],
+        (ids, *[hbm(v) for v in (w_qkv, tokens, *vectors)]),
+        scratch=[pltpu.VMEM(v.shape, BF) for v in (w_qkv, *vectors)] + [pltpu.SemaphoreType.DMA((11,))],
+        space=pltpu.HBM, micros=2.2)
+    moved_tokens = exchange(tokens, tokens_extra, "tokens")
+    one, two, out = call(
+        pick_mlp,
+        [struct((320, 1024), BF), struct((320, 1024), BF), struct((64, 1024), BF)],
+        (ids, hbm(after(w_fc1, a)), hbm(w_fc2), hbm(w_out)),
+        scratch=[pltpu.SemaphoreType.DMA((12,))],
+        space=pltpu.HBM, micros=1.9)
+    pieces = [a, fshift(a, 2, "qkv_x"), fshift(a, 4, "qkv_y"), fshift(a, 6, "qkv_xy")]
+    pieces.append(fshift(stack(ids, after(a, *moved_tokens, out), *pieces[1:]), 1, "qkv_core"))
+
+    one_x = fshift(after(one, moved_tokens[0]), 2, "one_x")
+    two_y = fshift(after(two, moved_tokens[0]), 4, "two_y")
+    out_xy = fshift(after(out, *pieces[1:4]), 6, "out_xy")
+
+    x, qkv, h1_e, h1_o, par = call(
+        qkv_body,
+        [
+            struct((rows, width), BF),
+            struct((rows, 1536), BF),
+            struct((rows, 512), BF),
+            struct((rows, 512), BF),
+            struct((8, 1536), F32),
+        ],
+        (ids, tokens, *moved_tokens, *pieces),
+        scratch=[pltpu.VMEM((rows, 1024), BF), pltpu.VMEM((1, 1536), F32)], micros=6.8)
+    one_two, two_two, outs_even = call(
+        stack_mlp_body,
+        [struct((512, 1024), BF), struct((512, 1024), BF), struct((256, 1024), BF)],
+        (ids, after(one, qkv), one_x, two, two_y, out_xy), micros=0.8)
+    outs_odd = fshift(outs_even, 1, "out_core")
+    valid = segment_ids >= 0
+    gm_own = jnp.where(valid[:, None], after(cotangent, *moved_tokens), jnp.zeros_like(cotangent))
+    valid_lanes = jnp.broadcast_to(valid[:, None].astype(F32), (own_rows, 128))
+    moved_gm = exchange(gm_own, gm_own[cut:], "cotangent")
+
+    def columns(base, size=rows):
+        return pl.BlockSpec((size, 128), lambda j: (0, base + j))
+
+    heads_o = pl.pallas_call(
+        partial(attend_body, own_rows, rows // 2),
+        grid=(4,),
+        out_shape=struct((rows, 512), BF),
+        in_specs=[SMEM_SPEC, columns(0), columns(4), columns(8)],
+        out_specs=columns(0),
+        compiler_params=pltpu.CompilerParams(vmem_limit_bytes=20 * 2**20),
+        cost_estimate=cost(7.1),
+    )(ids, after(qkv, one_two), qkv, qkv)
+    sizes = (320, rows - 320)
+
+    mine_0, mine_1, w_out_full = call(
+        mixed_body,
+        [struct((sizes[0], width), BF), struct((sizes[1], width), BF), struct((512, width), BF)],
+        (ids, heads_o, outs_even, outs_odd), micros=1.4)
+    theirs_0 = zshift(mine_0, PAIR, "mixed")
+    theirs_1 = zshift(after(mine_1, mine_0), PAIR, "mixed")
+    gm = call(place_grad_body, struct((rows, width), BF), (ids, after(gm_own, mine_1), *moved_gm), micros=1.0)
+    one_even = stack(ids, after(one_two, gm), fshift(one_two, 4, "one_y"))
+    two_even = stack(ids, after(two_two, gm), fshift(two_two, 2, "two_x"))
+    weights = (one_even, fshift(one_even, 1, "one_core"), two_even, fshift(two_even, 1, "two_core"))
+
+    def mlp(chunk, mine, theirs):
+        part = sizes[chunk]
+        return call(
+            partial(mlp_body, chunk * sizes[0]),
+            [
+                struct((part, 1024), F32),
+                struct((part, 512), BF),
+                struct((part, 512), BF),
+                struct((part, 1024), BF),
+                struct((part, 1024), BF),
+                struct((part, 2048), BF),
+                struct((part, 1024), BF),
+                struct((8, 256), F32),
+            ],
+            (ids, par, x, mine, theirs, gm, *weights),
+            scratch=[pltpu.VMEM((part, 1024), BF), pltpu.VMEM((part, 256), F32), pltpu.VMEM((part, 256), F32)], micros=11.2)
+
+    mid_0, h2_e0, h2_o0, act_e0, act_o0, gu_0, gh2_0, fc1_sums_0 = mlp(0, mine_0, theirs_0)
+    gh2_theirs_0 = zshift(gh2_0, PAIR, "mlp_grad")
+    mid_1, h2_e1, h2_o1, act_e1, act_o1, gu_1, gh2_1, fc1_sums_1 = mlp(1, after(mine_1, gh2_0), theirs_1)
+    gh2_theirs_1 = zshift(gh2_1, PAIR, "mlp_grad")
+
+    def row_grad(l0, l1, r0, r1, step):
+        return call(
+            partial(rows_grad_body, step),
+            struct((l0.shape[1], r0.shape[1]), BF),
+            (ids, l0, l1, r0, r1), micros=2.4)
+
+    send_two = row_grad(after(act_o0, gh2_1), act_o1, gm, gm, 256)
+    got_two = fshift(send_two, 1, "two_grad_core")
+    keep_two = row_grad(after(act_e0, send_two), act_e1, gm, gm, 256)
+    send_one = row_grad(after(h2_o0, keep_two), h2_o1, gu_0, gu_1, 512)
+    got_one = fshift(send_one, 1, "one_grad_core")
+    stay_two, send_two = merge(ids, [(after(keep_two, send_one), got_two, 0, 1024)])
+    got_two = fshift(send_two, 2, "two_grad_x")
+    keep_one = row_grad(after(h2_e0, stay_two), h2_e1, gu_0, gu_1, 512)
+    stay_one, send_one = merge(ids, [(keep_one, got_one, 0, 512)])
+    got_one = fshift(send_one, 4, "one_grad_y")
+
+    def middle_back(chunk, mid, mine, theirs):
+        part = sizes[chunk]
+        return call(
+            partial(middle_back_body, chunk * sizes[0]),
+            [struct((part, 1024), BF), struct((part, 512), BF), struct((8, 512), F32)],
+            (ids, par, mid, gm, mine, theirs, w_out_full), micros=4.0)
+
+    gb_0, go_0, mid_sums_0 = middle_back(0, after(mid_0, stay_one), gh2_0, gh2_theirs_0)
+    y_keep, y_send = call(
+        out_body,
+        [struct((own_rows, width), BF)] * 2,
+        (ids, after(act_e0, gb_0), act_o0, act_e1, act_o1, two_even, weights[3]),
+        scratch=[pltpu.VMEM((rows, width), BF)], micros=3.6)
+    y_theirs = zshift(after(y_send, gh2_theirs_1), PAIR, "output")
+    gb_1, go_1, mid_sums_1 = middle_back(1, after(mid_1, y_keep), gh2_1, gh2_theirs_1)
+    keep_o, send_o = call(
+        out_grad_body,
+        [struct((256, 1024), BF)] * 2,
+        (ids, heads_o, gb_0, gb_1),
+        scratch=[pltpu.VMEM((512, 1024), BF)], micros=1.7)
+    got_o = fshift(send_o, 1, "out_grad_core")
+    gq, gk, gv = pl.pallas_call(
+        partial(attend_back_body, own_rows, rows),
+        grid=(4,),
+        out_shape=[struct((rows, 512), BF)] * 3,
+        in_specs=[SMEM_SPEC, columns(0), columns(4), columns(8), columns(0, sizes[0]), columns(0, sizes[1])],
+        out_specs=[columns(0)] * 3,
+        compiler_params=pltpu.CompilerParams(vmem_limit_bytes=24 * 2**20),
+        cost_estimate=cost(14.0),
+    )(ids, qkv, qkv, qkv, after(go_0, keep_o), go_1)
+    stay_o, send_o = merge(ids, [(after(keep_o, gq), got_o, 0, 256)])
+    got_o = fshift(send_o, 2, "out_grad_x")
+    stay_one, send_one = merge(ids, [(after(stay_one, stay_o), got_one, 0, 256)])
+    got_one = fshift(send_one, 2, "one_grad_x")
+    result, result_extra = call(
+        result_body,
+        [struct((own_rows, width), BF), struct((cut, width), BF)],
+        (ids, par, mid_0, mid_1, after(y_keep, stay_one), y_theirs), micros=1.1)
+    result_extra = zshift(result_extra, ((3, 1),), "output_rows")
+
+    gh1_keep, gh1_send, one_sums = call(
+        input_grad_body,
+        [struct((own_rows, 1024), BF), struct((own_rows, 1024), BF), struct((8, 256), F32)],
+        (ids, x, par, gq, gk, after(gv, result), *pieces),
+        scratch=[pltpu.VMEM((rows, 1024), F32), pltpu.VMEM((rows, 1024), BF)], micros=7.0)
+    gh1_theirs = zshift(gh1_send, PAIR, "input_grad")
+    stay_two, send_two = merge(
+        ids, [(after(stay_two, gh1_send), got_two, 0, 512), (stay_o, got_o, 0, 128)]
+    )
+    got_two = fshift(send_two, 4, "two_grad_y")
+    keep_q, send_q = call(
+        qkv_grad_body,
+        [struct((576, 1536), BF), struct((576, 1536), BF)],
+        (ids, h1_e, h1_o, gq, gk, after(gv, stay_two), one_sums, mid_sums_0, mid_sums_1, fc1_sums_0, fc1_sums_1),
+        scratch=[pltpu.VMEM((8, 1536), F32)], micros=3.3)
+    got_q = fshift(send_q, 1, "qkv_grad_core")
+    stay_a, send_a, stay_b, send_b = merge(ids, [(keep_q, got_q, 0, 256)], [(keep_q, got_q, 256, 320)])
+    got_a = fshift(send_a, 2, "qkv_grad_x")
+    got_b = fshift(send_b, 4, "qkv_grad_y")
+    mlp_own, *mlp_sends = call(
+        line_mlp_body,
+        [struct((576, 256), BF)] * 4,
+        (ids, after(stay_two, stay_a), got_two, stay_one, got_one),
+        scratch=[pltpu.VMEM((320, 1024), BF), pltpu.VMEM((128, 2048), BF)], micros=1.2)
+    mlp_gots = [zshift(t, p, "mlp_grad_z") for t, p in zip(mlp_sends, (PAIR, FAR, CROSS))]
+    layer_output = call(
+        owner_rows_body,
+        struct((own_rows, width), BF),
+        (ids, valid_lanes, after(result, mlp_own), result_extra), micros=1.5)
+    back, back_extra = call(
+        input_back_body,
+        [struct((own_rows, width), F32), struct((cut, width), BF)],
+        (ids, par, x, gb_0, gb_1, after(gh1_keep, layer_output), gh1_theirs),
+        scratch=[pltpu.VMEM((rows, width), BF)], micros=4.0)
+    back_extra = zshift(back_extra, ((3, 1),), "input_grad_rows")
+    stay_a, send_a, stay_b, send_b = merge(
+        ids, [(after(stay_a, back), got_a, 0, 128)], [(stay_b, got_b, 0, 160)]
+    )
+    got_a = fshift(send_a, 4, "qkv_grad_y")
+    got_b = fshift(send_b, 2, "qkv_grad_x")
+    w_fc1_grad, w_fc2_grad, w_out_grad = call(
+        join_mlp_body,
+        [struct((128, 1024), F32), struct((512, 256), F32), struct((128, 256), F32)],
+        (ids, after(mlp_own, stay_a), *mlp_gots), micros=1.7)
+    own, to_pair, to_far, to_cross = call(
+        line_body,
+        [struct((192, 384), BF)] * 4,
+        (ids, after(stay_a, w_out_grad), got_a, stay_b, got_b),
+        scratch=[pltpu.VMEM((64, 1536), BF), pltpu.VMEM((80, 1536), BF)], micros=0.8)
+    got_pair = zshift(to_pair, PAIR, "qkv_grad_z")
+    got_far = zshift(to_far, FAR, "qkv_grad_z")
+    got_cross = zshift(to_cross, CROSS, "qkv_grad_z")
+    tokens_grad = call(
+        owner_rows_body,
+        struct((own_rows, width), F32),
+        (ids, valid_lanes, after(back, own), back_extra), micros=1.5)
+    w_qkv_grad, sums = call(
+        join_body,
+        [struct((128, 768), F32), struct((9, 128), F32)],
+        (ids, own, got_pair, got_far, got_cross),
+        scratch=[pltpu.VMEM((4, 128), F32)], micros=1.4)
+
+    def vector(spot):
+        return sums[spot, 0:32]
+
+    return (
+        layer_output,
+        tokens_grad,
+        vector(0),
+        vector(1),
+        w_qkv_grad,
+        vector(6),
+        vector(7),
+        w_out_grad,
+        vector(2),
+        vector(3),
+        vector(4),
+        w_fc1_grad,
+        sums[8],
+        w_fc2_grad,
+        vector(5),
+    )
+
+
+def shards(*operands):
+    tokens = operands[0]
+    fits = (
+        lax.axis_size("fsdp") == 8
+        and lax.axis_size("seq") == 4
+        and tokens.shape == (384, 1024)
+        and operands[11].shape == (128, 4096)
+    )
+    return paired_shards(*operands) if fits else general_shards(*operands)
 
 
 def solution(mesh):

time: 865 us -> 289 us (0.33)
  matrix products: 265 us -> 0 us
  blocking collectives: 190 us -> 0 us
  Pallas kernels: 0 us -> 112 us
  local copies, waits for them, and re-layouts: 110 us -> 1.2 us
  other arithmetic: 83.1 us -> 0.13 us
  waiting for transfers between devices: 160 us -> 89.9 us
  starting transfers between devices: 18.5 us -> 79 us
  between operations: 17.6 us -> 1.59 us
  loops' own time: 13.8 us -> 0 us
    dot_general x26 -> x0, matrix products: 265 us -> none  [the longest x4 50.5 us: block_scores(): jnp.einsum('qhd,khd->hqk', query_block, key_window, preferred_element_typ...]
    all_gather x10 -> x0, blocking collectives: 154 us -> none  [the longest x1 75.7 us: shards(): span_labels = lax.all_gather(segment_ids, 'seq', axis=0, tiled=True)]
    pallas_call x0 -> x38, Pallas kernels: none -> 112 us  [the longest x36 90.9 us: call(): pl.pallas_call(body, out_shape=shapes, in_specs=[SMEM_SPEC] + [pl.BlockSp...]
    ppermute x0 -> x45, waiting for transfers between devices: none -> 89.9 us  [the longest x20 61.9 us: zshift(): return lax.ppermute(values, 'seq', pairs)]
    all_to_all x4 -> x0, waiting for transfers between devices: 84 us -> none  [the longest x1 73.3 us: shards(): lax.all_to_all(head_grads, 'seq', split_axis=0, concat_axis=2, tiled=True)]
    ppermute x0 -> x45, starting transfers between devices: none -> 79 us  [the longest x20 58.9 us: zshift(): return lax.ppermute(values, 'seq', pairs)]
    reduce_scatter x8 -> x0, waiting for transfers between devices: 59.9 us -> none  [the longest x1 28.8 us: shards(): lax.psum_scatter(w_qkv_part.astype(jnp.bfloat16), 'fsdp', scatter_dimensi...]
    convert_element_type x21 -> x1, other arithmetic: 44.7 us -> 0.01 us  [paired_shards(): valid_lanes = jnp.broadcast_to(valid[:, None].astype(F32), (own_rows, 128))]
  transfers between devices with their start and end apart: 16 -> 45, of which waited for: 6 -> 15; matrix products, arithmetic and copies ran while one was open for 49% -> 0% of each run, Pallas kernels for 0% -> 32%
where the time goes in v1:
time: 289 us; the launch traced here: 284 us
  Pallas kernels  112 us (39%)
  waiting for transfers between devices  89.9 us (31%)
  starting transfers between devices  79 us (27%)
    pallas_call x36, Pallas kernels, call(): pl.pallas_call(body, out_shape=shapes, in_specs=[SMEM_SPEC] + [pl.BlockSp...  90.9 us
    ppermute x20, waiting for transfers between devices, zshift(): return lax.ppermute(values, 'seq', pairs)  61.9 us
    ppermute x20, starting transfers between devices, zshift(): return lax.ppermute(values, 'seq', pairs)  58.9 us
    ppermute x25, waiting for transfers between devices, fshift(): return lax.ppermute(values, 'fsdp', [(i, i ^ bit) for i in range(8)])  28.1 us
    ppermute x25, starting transfers between devices, fshift(): return lax.ppermute(values, 'fsdp', [(i, i ^ bit) for i in range(8)])  20.1 us
    pallas_call x1, Pallas kernels, paired_shards(): pl.pallas_call(partial(attend_back_body, own_rows, rows), grid=(4,), out_...  14.2 us
    pallas_call x1, Pallas kernels, paired_shards(): pl.pallas_call(partial(attend_body, own_rows, rows // 2), grid=(4,), out_...  7.17 us
  transfers between devices with their start and end apart: 45, of which 15 were waited for; matrix products, arithmetic and copies ran while one was open for 0% of the time, Pallas kernels for 32%

profile of v1, /device:TPU:0, one launch (start us, length us, event | category | flops | bytes accessed | tf_op | source)
XLA Modules:
  0.0 284.2 jit_solution(10952223485090240966)
XLA Ops:
  3.6 5.9 %collective-permute-start = (bf16[384,1024]{1,0:T(8,128)(2,1)}, bf16[384,1024]{1,0:T(8,128)(2,1)S(1)}, u32[]{:S(2)}, u32[]{:S(2)}) collective-permute-start(bf16[384,1024]{1,0:T(8,128)(2,1)} %own_ref.1), channel_id=1, source_target_pairs={{0,1},{1,0},{2,3},{3,2},{4,5},{5,4},{6,7},{7,6},{8,9},{9,8},{10,11... | collective-permute-start | bytes 2359304 | tf_op jit(solution)/shard_map/tokens/ppermute | solution.py:376
  15.6 11.4 %collective-permute-done.theirs_ref = bf16[384,1024]{1,0:T(8,128)(2,1)S(1)} collective-permute-done((bf16[384,1024]{1,0:T(8,128)(2,1)}, bf16[384,1024]{1,0:T(8,128)(2,1)S(1)}, u32[]{:S(2)}, u32[]{:S(2)}) %collective-permute-start) | collective-permute-done | bytes 786464 | tf_op jit(solution)/shard_map/tokens/ppermute | solution.py:376
  27.0 4.6 %collective-permute-done.4.refs_2_ = bf16[144,1536]{1,0:T(8,128)(2,1)S(1)} collective-permute-done((bf16[144,1536]{1,0:T(8,128)(2,1)S(1)}, bf16[144,1536]{1,0:T(8,128)(2,1)S(1)}, u32[]{:S(2)}, u32[]{:S(2)}) %collective-permute-start.4) | collective-permute-done | bytes 442400 | tf_op jit(solution)/shard_map/qkv_y/ppermute | solution.py:371
  35.9 6.8 %shard_map.274 = (bf16[608,1024]{1,0:T(8,128)(2,1)S(1)}, bf16[608,1536]{1,0:T(8,128)(2,1)S(1)}, bf16[608,512]{1,0:T(8,128)(2,1)S(1)}, bf16[608,512]{1,0:T(8,128)(2,1)S(1)}, f32[8,1536]{1,0:T(8,128)S(1)}) custom-call(s32[2]{0:T(128)S(1)} %compare_select_fusion.ids, bf16[384,1024]{1,0:T(8,128)(2,1)S(1)} %copy-done, ...), custom_call_target="tpu_custom_call" | custom-call | flops 680000000 | bytes 1 | tf_op jit(solution)/shard_map/pallas_call | solution.py:390
  42.7 10.4 %collective-permute-done.9.out_ref = bf16[64,1024]{1,0:T(8,128)(2,1)S(1)} collective-permute-done((bf16[64,1024]{1,0:T(8,128)(2,1)S(1)}, bf16[64,1024]{1,0:T(8,128)(2,1)S(1)}, u32[]{:S(2)}, u32[]{:S(2)}) %collective-permute-start.9) | collective-permute-done | bytes 131104 | tf_op jit(solution)/shard_map/out_xy/ppermute | solution.py:371
  57.1 5.1 %collective-permute-start.12 = (bf16[384,1024]{1,0:T(8,128)(2,1)S(1)}, bf16[384,1024]{1,0:T(8,128)(2,1)S(1)}, u32[]{:S(2)}, u32[]{:S(2)}) collective-permute-start(bf16[384,1024]{1,0:T(8,128)(2,1)S(1)} %broadcast_select_fusion.own_ref), channel_id=1, source_target_pairs={{0,1},{1,0},{2,3},{3,2},{4,5},{5,4},{6,7},{7,6},{8,9},{9,8},{10,11... | collective-permute-start | bytes 2359304 | tf_op jit(solution)/shard_map/cotangent/ppermute | solution.py:376
  62.9 7.2 %shard_map.276.o_ref = bf16[608,512]{1,0:T(8,128)(2,1)S(1)} custom-call(s32[2]{0:T(128)S(1)} %compare_select_fusion.ids, bf16[608,1536]{1,0:T(8,128)(2,1)S(1)} %get-tuple-element.151.q_ref.k_ref.v_ref, bf16[608,1536]{1,0:T(8,128)(2,1)S(1)} %get-tuple-element.151.q_ref.k_ref.v_ref, bf16[608,1536]{1,0:T(8,128)(2,1)S(1)} %get-tuple-element.151.q_ref.k_ref.v_ref), custom_call_target="tpu_custom_call" | custom-call | flops 710000000 | bytes 1 | tf_op jit(solution)/shard_map/pallas_call | solution.py:1174
  71.5 7.0 %collective-permute-done.12.theirs_ref = bf16[384,1024]{1,0:T(8,128)(2,1)S(1)} collective-permute-done((bf16[384,1024]{1,0:T(8,128)(2,1)S(1)}, bf16[384,1024]{1,0:T(8,128)(2,1)S(1)}, u32[]{:S(2)}, u32[]{:S(2)}) %collective-permute-start.12) | collective-permute-done | bytes 786464 | tf_op jit(solution)/shard_map/cotangent/ppermute | solution.py:376
  83.4 15.6 %collective-permute-done.11.theirs_ref = bf16[320,1024]{1,0:T(8,128)(2,1)S(1)} collective-permute-done((bf16[320,1024]{1,0:T(8,128)(2,1)S(1)}, bf16[320,1024]{1,0:T(8,128)(2,1)S(1)}, u32[]{:S(2)}, u32[]{:S(2)}) %collective-permute-start.11) | collective-permute-done | bytes 655392 | tf_op jit(solution)/shard_map/mixed/ppermute | solution.py:376
  99.0 11.5 %shard_map.281 = (f32[320,1024]{1,0:T(8,128)S(1)}, bf16[320,512]{1,0:T(8,128)(2,1)S(1)}, bf16[320,512]{1,0:T(8,128)(2,1)S(1)}, bf16[320,1024]{1,0:T(8,128)(2,1)S...) custom-call(s32[2]{0:T(128)S(1)} %compare_select_fusion.ids, ...), custom_call_target="tpu_custom_call" | custom-call | flops 1120000000 | bytes 1 | tf_op jit(solution)/shard_map/pallas_call | solution.py:390
  110.8 10.8 %shard_map.282 = (f32[288,1024]{1,0:T(8,128)S(1)}, bf16[288,512]{1,0:T(8,128)(2,1)S(1)}, bf16[288,512]{1,0:T(8,128)(2,1)S(1)}, bf16[288,1024]{1,0:T(8,128)(2,1)S...) custom-call(s32[2]{0:T(128)S(1)} %compare_select_fusion.ids, ...), custom_call_target="tpu_custom_call" | custom-call | flops 1120000000 | bytes 1 | tf_op jit(solution)/shard_map/pallas_call | solution.py:390
  137.9 9.0 %collective-permute-done.22.theirs_ref = bf16[320,1024]{1,0:T(8,128)(2,1)S(1)} collective-permute-done((bf16[320,1024]{1,0:T(8,128)(2,1)S(1)}, bf16[320,1024]{1,0:T(8,128)(2,1)S(1)}, u32[]{:S(2)}, u32[]{:S(2)}) %collective-permute-start.22) | collective-permute-done | bytes 655392 | tf_op jit(solution)/shard_map/mlp_grad/ppermute | solution.py:376
  147.0 4.2 %shard_map.289 = (bf16[320,1024]{1,0:T(8,128)(2,1)S(1)}, bf16[320,512]{1,0:T(8,128)(2,1)S(1)}, f32[8,512]{1,0:T(8,128)S(1)}) custom-call(s32[2]{0:T(128)S(1)} %compare_select_fusion.ids, f32[8,1536]{1,0:T(8,128)S(1)} %get-tuple-element.141.par_ref, f32[320,1024]{1,0:T(8,128)S(1)} %get-tuple-element.183.mid_ref.mid0_ref, ...), custom_call_target="tpu_custom_call" | custom-call | flops 400000000 | bytes 1 | tf_op jit(solution)/shard_map/pallas_call | solution.py:390
  154.7 4.0 %collective-permute-done.23.theirs_ref = bf16[288,1024]{1,0:T(8,128)(2,1)S(1)} collective-permute-done((bf16[288,1024]{1,0:T(8,128)(2,1)S(1)}, bf16[288,1024]{1,0:T(8,128)(2,1)S(1)}, u32[]{:S(2)}, u32[]{:S(2)}) %collective-permute-start.23) | collective-permute-done | bytes 589856 | tf_op jit(solution)/shard_map/mlp_grad/ppermute | solution.py:376
  160.5 3.8 %shard_map.291 = (bf16[288,1024]{1,0:T(8,128)(2,1)S(1)}, bf16[288,512]{1,0:T(8,128)(2,1)S(1)}, f32[8,512]{1,0:T(8,128)S(1)}) custom-call(s32[2]{0:T(128)S(1)} %compare_select_fusion.ids, f32[8,1536]{1,0:T(8,128)S(1)} %get-tuple-element.141.par_ref, f32[288,1024]{1,0:T(8,128)S(1)} %get-tuple-element.188.mid_ref.mid1_ref, ...), custom_call_target="tpu_custom_call" | custom-call | flops 400000000 | bytes 1 | tf_op jit(solution)/shard_map/pallas_call | solution.py:390
  166.0 14.2 %shard_map.293 = (bf16[608,512]{1,0:T(8,128)(2,1)S(1)}, bf16[608,512]{1,0:T(8,128)(2,1)S(1)}, bf16[608,512]{1,0:T(8,128)(2,1)S(1)}) custom-call(s32[2]{0:T(128)S(1)} %compare_select_fusion.ids, bf16[608,1536]{1,0:T(8,128)(2,1)S(1)} %get-tuple-element.151.q_ref.k_ref.v_ref, bf16[608,1536]{1,0:T(8,128)(2,1)S(1)} %get-tuple-element.151.q_ref.k_ref.v_ref, ...), custom_call_target="tpu_custom_call" | custom-call | flops 1400000000 | bytes 1 | tf_op jit(solution)/shard_map/pallas_call | solution.py:1256
  184.3 7.0 %shard_map.297 = (bf16[384,1024]{1,0:T(8,128)(2,1)S(1)}, bf16[384,1024]{1,0:T(8,128)(2,1)S(1)}, f32[8,256]{1,0:T(8,128)S(1)}) custom-call(s32[2]{0:T(128)S(1)} %compare_select_fusion.ids, bf16[608,1024]{1,0:T(8,128)(2,1)S(1)} %get-tuple-element.142.x_ref, f32[8,1536]{1,0:T(8,128)S(1)} %get-tuple-element.141.par_ref, ...), custom_call_target="tpu_custom_call" | custom-call | flops 700000000 | bytes 1 | tf_op jit(solution)/shard_map/pallas_call | solution.py:390
  201.5 8.3 %collective-permute-done.31.r1_ref = bf16[128,2048]{1,0:T(8,128)(2,1)S(1)} collective-permute-done((bf16[128,2048]{1,0:T(8,128)(2,1)S(1)}, bf16[128,2048]{1,0:T(8,128)(2,1)S(1)}, u32[]{:S(2)}, u32[]{:S(2)}) %collective-permute-start.31) | collective-permute-done | bytes 524320 | tf_op jit(solution)/shard_map/one_grad_x/ppermute | solution.py:371
  215.5 9.4 %collective-permute-start.37 = (bf16[576,256]{1,0:T(8,128)(2,1)S(1)}, bf16[576,256]{1,0:T(8,128)(2,1)S(1)}, u32[]{:S(2)}, u32[]{:S(2)}) collective-permute-start(bf16[576,256]{1,0:T(8,128)(2,1)S(1)} %get-tuple-element.240), channel_id=1, source_target_pairs={{0,2},{2,0},{1,3},{3,1},{4,6},{6,4},{5,7},{7,5},{8,10},{10,8},{9,1... | collective-permute-start | bytes 884744 | tf_op jit(solution)/shard_map/mlp_grad_z/ppermute | solution.py:376
  224.9 13.5 %collective-permute-start.38 = (bf16[576,256]{1,0:T(8,128)(2,1)S(1)}, bf16[576,256]{1,0:T(8,128)(2,1)S(1)}, u32[]{:S(2)}, u32[]{:S(2)}) collective-permute-start(bf16[576,256]{1,0:T(8,128)(2,1)S(1)} %get-tuple-element.241), channel_id=1, source_target_pairs={{0,3},{3,0},{1,2},{2,1},{4,7},{7,4},{5,6},{6,5},{8,11},{11,8},{9,1... | collective-permute-start | bytes 884744 | tf_op jit(solution)/shard_map/mlp_grad_z/ppermute | solution.py:376
  240.1 4.1 %shard_map.303 = (f32[384,1024]{1,0:T(8,128)S(1)}, bf16[192,1024]{1,0:T(8,128)(2,1)S(1)}) custom-call(s32[2]{0:T(128)S(1)} %compare_select_fusion.ids, f32[8,1536]{1,0:T(8,128)S(1)} %get-tuple-element.141.par_ref, bf16[608,1024]{1,0:T(8,128)(2,1)S(1)} %get-tuple-element.142.x_ref, bf16[320,1024]{1,0:T(8,128)(2,1)S(1)} %get-tuple-element.185.gb0_ref, ...), custom_call_target="tpu_custom_call" | custom-call | flops 400000000 | bytes 1 | tf_op jit(solution)/shard_map/pallas_call | solution.py:390
  247.8 6.8 %collective-permute-done.38.cross_ref = bf16[576,256]{1,0:T(8,128)(2,1)S(1)} collective-permute-done((bf16[576,256]{1,0:T(8,128)(2,1)S(1)}, bf16[576,256]{1,0:T(8,128)(2,1)S(1)}, u32[]{:S(2)}, u32[]{:S(2)}) %collective-permute-start.38) | collective-permute-done | bytes 294944 | tf_op jit(solution)/shard_map/mlp_grad_z/ppermute | solution.py:376
  257.0 12.0 %collective-permute-start.42 = (bf16[192,384]{1,0:T(8,128)(2,1)S(1)}, bf16[192,384]{1,0:T(8,128)(2,1)S(1)}, u32[]{:S(2)}, u32[]{:S(2)}) collective-permute-start(bf16[192,384]{1,0:T(8,128)(2,1)S(1)} %get-tuple-element.250), channel_id=1, source_target_pairs={{0,1},{1,0},{2,3},{3,2},{4,5},{5,4},{6,7},{7,6},{8,9},{9,8},{10,11... | collective-permute-start | bytes 442376 | tf_op jit(solution)/shard_map/qkv_grad_z/ppermute | solution.py:376
  274.4 6.7 %collective-permute-done.43.far_ref = bf16[192,384]{1,0:T(8,128)(2,1)S(1)} collective-permute-done((bf16[192,384]{1,0:T(8,128)(2,1)S(1)}, bf16[192,384]{1,0:T(8,128)(2,1)S(1)}, u32[]{:S(2)}, u32[]{:S(2)}) %collective-permute-start.43) | collective-permute-done | bytes 147488 | tf_op jit(solution)/shard_map/qkv_grad_z/ppermute | solution.py:376
  (117 shorter events, 83.4 us)
Async XLA Ops:
  3.6 23.4 %collective-permute-start = (bf16[384,1024]{1,0:T(8,128)(2,1)}, bf16[384,1024]{1,0:T(8,128)(2,1)S(1)}, u32[]{:S(2)}, u32[]{:S(2)}) collective-permute-start(bf16[384,1024]{1,0:T(8,128)(2,1)} %own_ref.1), channel_id=1, source_target_pairs={{0,1},{1,0},{2,3},{3,2},{4,5},{5,4},{6,7},{7,6},{8,9},{9,8},{10,11... | collective-permute-start | bytes 2359304 | tf_op jit(solution)/shard_map/tokens/ppermute | solution.py:376
  11.0 20.5 %collective-permute-start.4 = (bf16[144,1536]{1,0:T(8,128)(2,1)S(1)}, bf16[144,1536]{1,0:T(8,128)(2,1)S(1)}, u32[]{:S(2)}, u32[]{:S(2)}) collective-permute-start(bf16[144,1536]{1,0:T(8,128)(2,1)S(1)} %get-tuple-element.140.refs_0_), channel_id=1, source_target_pairs={{0,16},{4,20},{8,24},{12,28},{16,0},{20,4},{24,8},{28,12},{1,17},{... | collective-permute-start | bytes 1327112 | tf_op jit(solution)/shard_map/qkv_y/ppermute | solution.py:371
  12.5 19.0 %collective-permute-start.5 = (bf16[144,1536]{1,0:T(8,128)(2,1)S(1)}, bf16[144,1536]{1,0:T(8,128)(2,1)S(1)}, u32[]{:S(2)}, u32[]{:S(2)}) collective-permute-start(bf16[144,1536]{1,0:T(8,128)(2,1)S(1)} %get-tuple-element.140.refs_0_), channel_id=1, source_target_pairs={{0,24},{4,28},{8,16},{12,20},{16,8},{20,12},{24,0},{28,4},{1,25},{... | collective-permute-start | bytes 1327112 | tf_op jit(solution)/shard_map/qkv_xy/ppermute | solution.py:371
  32.3 20.9 %collective-permute-start.7 = (bf16[320,1024]{1,0:T(8,128)(2,1)S(1)}, bf16[320,1024]{1,0:T(8,128)(2,1)S(1)}, u32[]{:S(2)}, u32[]{:S(2)}) collective-permute-start(bf16[320,1024]{1,0:T(8,128)(2,1)S(1)} %get-tuple-element.146.one_ref), channel_id=1, source_target_pairs={{0,8},{4,12},{8,0},{12,4},{16,24},{20,28},{24,16},{28,20},{1,9},{5... | collective-permute-start | bytes 1966088 | tf_op jit(solution)/shard_map/one_x/ppermute | solution.py:371
  33.6 19.6 %collective-permute-start.8 = (bf16[320,1024]{1,0:T(8,128)(2,1)S(1)}, bf16[320,1024]{1,0:T(8,128)(2,1)S(1)}, u32[]{:S(2)}, u32[]{:S(2)}) collective-permute-start(bf16[320,1024]{1,0:T(8,128)(2,1)S(1)} %get-tuple-element.148.two_ref), channel_id=1, source_target_pairs={{0,16},{4,20},{8,24},{12,28},{16,0},{20,4},{24,8},{28,12},{1,17},{... | collective-permute-start | bytes 1966088 | tf_op jit(solution)/shard_map/two_y/ppermute | solution.py:371
  34.4 18.8 %collective-permute-start.9 = (bf16[64,1024]{1,0:T(8,128)(2,1)S(1)}, bf16[64,1024]{1,0:T(8,128)(2,1)S(1)}, u32[]{:S(2)}, u32[]{:S(2)}) collective-permute-start(bf16[64,1024]{1,0:T(8,128)(2,1)S(1)} %get-tuple-element.149), channel_id=1, source_target_pairs={{0,24},{4,28},{8,16},{12,20},{16,8},{20,12},{24,0},{28,4},{1,25},{... | collective-permute-start | bytes 393224 | tf_op jit(solution)/shard_map/out_xy/ppermute | solution.py:371
  53.9 25.5 %collective-permute-start.17 = (bf16[512,1024]{1,0:T(8,128)(2,1)S(1)}, bf16[512,1024]{1,0:T(8,128)(2,1)S(1)}, u32[]{:S(2)}, u32[]{:S(2)}) collective-permute-start(bf16[512,1024]{1,0:T(8,128)(2,1)S(1)} %get-tuple-element.159.refs_0_), channel_id=1, source_target_pairs={{0,8},{4,12},{8,0},{12,4},{16,24},{20,28},{24,16},{28,20},{1,9},{5... | collective-permute-start | bytes 3145736 | tf_op jit(solution)/shard_map/two_x/ppermute | solution.py:371
  54.7 25.4 %collective-permute-start.15 = (bf16[512,1024]{1,0:T(8,128)(2,1)S(1)}, bf16[512,1024]{1,0:T(8,128)(2,1)S(1)}, u32[]{:S(2)}, u32[]{:S(2)}) collective-permute-start(bf16[512,1024]{1,0:T(8,128)(2,1)S(1)} %get-tuple-element.157.refs_0_), channel_id=1, source_target_pairs={{0,16},{4,20},{8,24},{12,28},{16,0},{20,4},{24,8},{28,12},{1,17},{... | collective-permute-start | bytes 3145736 | tf_op jit(solution)/shard_map/one_y/ppermute | solution.py:371
  57.1 21.3 %collective-permute-start.12 = (bf16[384,1024]{1,0:T(8,128)(2,1)S(1)}, bf16[384,1024]{1,0:T(8,128)(2,1)S(1)}, u32[]{:S(2)}, u32[]{:S(2)}) collective-permute-start(bf16[384,1024]{1,0:T(8,128)(2,1)S(1)} %broadcast_select_fusion.own_ref), channel_id=1, source_target_pairs={{0,1},{1,0},{2,3},{3,2},{4,5},{5,4},{6,7},{7,6},{8,9},{9,8},{10,11... | collective-permute-start | bytes 2359304 | tf_op jit(solution)/shard_map/cotangent/ppermute | solution.py:376
  80.1 18.9 %collective-permute-start.18 = (bf16[1024,1024]{1,0:T(8,128)(2,1)S(1)}, bf16[1024,1024]{1,0:T(8,128)(2,1)S(1)}, u32[]{:S(2)}, u32[]{:S(2)}) collective-permute-start(bf16[1024,1024]{1,0:T(8,128)(2,1)S(1)} %shard_map.280.two_a), channel_id=1, source_target_pairs={{0,4},{4,0},{8,12},{12,8},{16,20},{20,16},{24,28},{28,24},{1,5},{5... | collective-permute-start | bytes 6291464 | tf_op jit(solution)/shard_map/two_core/ppermute | solution.py:371
  80.9 18.1 %collective-permute-start.16 = (bf16[1024,1024]{1,0:T(8,128)(2,1)S(1)}, bf16[1024,1024]{1,0:T(8,128)(2,1)S(1)}, u32[]{:S(2)}, u32[]{:S(2)}) collective-permute-start(bf16[1024,1024]{1,0:T(8,128)(2,1)S(1)} %shard_map.279.one_a), channel_id=1, source_target_pairs={{0,4},{4,0},{8,12},{12,8},{16,20},{20,16},{24,28},{28,24},{1,5},{5... | collective-permute-start | bytes 6291464 | tf_op jit(solution)/shard_map/one_core/ppermute | solution.py:371
  83.2 27.6 %collective-permute-start.19 = (bf16[288,1024]{1,0:T(8,128)(2,1)S(1)}, bf16[288,1024]{1,0:T(8,128)(2,1)S(1)}, u32[]{:S(2)}, u32[]{:S(2)}) collective-permute-start(bf16[288,1024]{1,0:T(8,128)(2,1)S(1)} %get-tuple-element.163.mine_ref), channel_id=1, source_target_pairs={{0,1},{1,0},{2,3},{3,2},{4,5},{5,4},{6,7},{7,6},{8,9},{9,8},{10,11... | collective-permute-start | bytes 1769480 | tf_op jit(solution)/shard_map/mixed/ppermute | solution.py:376
  131.1 27.6 %collective-permute-start.23 = (bf16[288,1024]{1,0:T(8,128)(2,1)S(1)}, bf16[288,1024]{1,0:T(8,128)(2,1)S(1)}, u32[]{:S(2)}, u32[]{:S(2)}) collective-permute-start(bf16[288,1024]{1,0:T(8,128)(2,1)S(1)} %get-tuple-element.168.mine_ref), channel_id=1, source_target_pairs={{0,1},{1,0},{2,3},{3,2},{4,5},{5,4},{6,7},{7,6},{8,9},{9,8},{10,11... | collective-permute-start | bytes 1769480 | tf_op jit(solution)/shard_map/mlp_grad/ppermute | solution.py:376
  135.8 46.6 %collective-permute-start.25 = (bf16[256,2048]{1,0:T(8,128)(2,1)S(1)}, bf16[256,2048]{1,0:T(8,128)(2,1)S(1)}, u32[]{:S(2)}, u32[]{:S(2)}) collective-permute-start(bf16[256,2048]{1,0:T(8,128)(2,1)S(1)} %get-tuple-element.199), channel_id=1, source_target_pairs={{0,16},{4,20},{8,24},{12,28},{16,0},{20,4},{24,8},{28,12},{1,17},{... | collective-permute-start | bytes 3145736 | tf_op jit(solution)/shard_map/one_grad_y/ppermute | solution.py:371
  137.3 54.0 %collective-permute-start.27 = (bf16[512,1024]{1,0:T(8,128)(2,1)S(1)}, bf16[512,1024]{1,0:T(8,128)(2,1)S(1)}, u32[]{:S(2)}, u32[]{:S(2)}) collective-permute-start(bf16[512,1024]{1,0:T(8,128)(2,1)S(1)} %get-tuple-element.210), channel_id=1, source_target_pairs={{0,8},{4,12},{8,0},{12,4},{16,24},{20,28},{24,16},{28,20},{1,9},{5... | collective-permute-start | bytes 3145736 | tf_op jit(solution)/shard_map/two_grad_x/ppermute | solution.py:371
  158.7 24.5 %collective-permute-start.26 = (bf16[384,1024]{1,0:T(8,128)(2,1)S(1)}, bf16[384,1024]{1,0:T(8,128)(2,1)S(1)}, u32[]{:S(2)}, u32[]{:S(2)}) collective-permute-start(bf16[384,1024]{1,0:T(8,128)(2,1)S(1)} %get-tuple-element.203), channel_id=1, source_target_pairs={{0,1},{1,0},{2,3},{3,2},{4,5},{5,4},{6,7},{7,6},{8,9},{9,8},{10,11... | collective-permute-start | bytes 2359304 | tf_op jit(solution)/shard_map/output/ppermute | solution.py:376
  196.3 17.6 %collective-permute-start.30 = (bf16[320,1024]{1,0:T(8,128)(2,1)S(1)}, bf16[320,1024]{1,0:T(8,128)(2,1)S(1)}, u32[]{:S(2)}, u32[]{:S(2)}) collective-permute-start(bf16[320,1024]{1,0:T(8,128)(2,1)S(1)} %get-tuple-element.225), channel_id=1, source_target_pairs={{0,16},{4,20},{8,24},{12,28},{16,0},{20,4},{24,8},{28,12},{1,17},{... | collective-permute-start | bytes 1966088 | tf_op jit(solution)/shard_map/two_grad_y/ppermute | solution.py:371
  197.8 27.1 %collective-permute-start.33 = (bf16[384,1024]{1,0:T(8,128)(2,1)S(1)}, bf16[384,1024]{1,0:T(8,128)(2,1)S(1)}, u32[]{:S(2)}, u32[]{:S(2)}) collective-permute-start(bf16[384,1024]{1,0:T(8,128)(2,1)S(1)} %get-tuple-element.208), channel_id=1, source_target_pairs={{0,1},{1,0},{2,3},{3,2},{4,5},{5,4},{6,7},{7,6},{8,9},{9,8},{10,11... | collective-permute-start | bytes 2359304 | tf_op jit(solution)/shard_map/input_grad/ppermute | solution.py:376
  200.2 44.8 %collective-permute-start.35 = (bf16[160,1536]{1,0:T(8,128)(2,1)S(1)}, bf16[160,1536]{1,0:T(8,128)(2,1)S(1)}, u32[]{:S(2)}, u32[]{:S(2)}) collective-permute-start(bf16[160,1536]{1,0:T(8,128)(2,1)S(1)} %get-tuple-element.236), channel_id=1, source_target_pairs={{0,16},{4,20},{8,24},{12,28},{16,0},{20,4},{24,8},{28,12},{1,17},{... | collective-permute-start | bytes 1474568 | tf_op jit(solution)/shard_map/qkv_grad_y/ppermute | solution.py:371
  209.9 34.4 %collective-permute-start.34 = (bf16[128,1536]{1,0:T(8,128)(2,1)S(1)}, bf16[128,1536]{1,0:T(8,128)(2,1)S(1)}, u32[]{:S(2)}, u32[]{:S(2)}) collective-permute-start(bf16[128,1536]{1,0:T(8,128)(2,1)S(1)} %get-tuple-element.234), channel_id=1, source_target_pairs={{0,8},{4,12},{8,0},{12,4},{16,24},{20,28},{24,16},{28,20},{1,9},{5... | collective-permute-start | bytes 1179656 | tf_op jit(solution)/shard_map/qkv_grad_x/ppermute | solution.py:371
  215.1 31.3 %collective-permute-start.36 = (bf16[576,256]{1,0:T(8,128)(2,1)S(1)}, bf16[576,256]{1,0:T(8,128)(2,1)S(1)}, u32[]{:S(2)}, u32[]{:S(2)}) collective-permute-start(bf16[576,256]{1,0:T(8,128)(2,1)S(1)} %get-tuple-element.239), channel_id=1, source_target_pairs={{0,1},{1,0},{2,3},{3,2},{4,5},{5,4},{6,7},{7,6},{8,9},{9,8},{10,11... | collective-permute-start | bytes 884744 | tf_op jit(solution)/shard_map/mlp_grad_z/ppermute | solution.py:376
  215.5 32.3 %collective-permute-start.37 = (bf16[576,256]{1,0:T(8,128)(2,1)S(1)}, bf16[576,256]{1,0:T(8,128)(2,1)S(1)}, u32[]{:S(2)}, u32[]{:S(2)}) collective-permute-start(bf16[576,256]{1,0:T(8,128)(2,1)S(1)} %get-tuple-element.240), channel_id=1, source_target_pairs={{0,2},{2,0},{1,3},{3,1},{4,6},{6,4},{5,7},{7,5},{8,10},{10,8},{9,1... | collective-permute-start | bytes 884744 | tf_op jit(solution)/shard_map/mlp_grad_z/ppermute | solution.py:376
  224.9 29.7 %collective-permute-start.38 = (bf16[576,256]{1,0:T(8,128)(2,1)S(1)}, bf16[576,256]{1,0:T(8,128)(2,1)S(1)}, u32[]{:S(2)}, u32[]{:S(2)}) collective-permute-start(bf16[576,256]{1,0:T(8,128)(2,1)S(1)} %get-tuple-element.241), channel_id=1, source_target_pairs={{0,3},{3,0},{1,2},{2,1},{4,7},{7,4},{5,6},{6,5},{8,11},{11,8},{9,1... | collective-permute-start | bytes 884744 | tf_op jit(solution)/shard_map/mlp_grad_z/ppermute | solution.py:376
  244.3 27.2 %collective-permute-start.41 = (bf16[192,1024]{1,0:T(8,128)(2,1)S(1)}, bf16[192,1024]{1,0:T(8,128)(2,1)S(1)}, u32[]{:S(2)}, u32[]{:S(2)}) collective-permute-start(bf16[192,1024]{1,0:T(8,128)(2,1)S(1)} %get-tuple-element.249), channel_id=1, source_target_pairs={{3,1},{7,5},{11,9},{15,13},{19,17},{23,21},{27,25},{31,29}} | collective-permute-start | bytes 1179656 | tf_op jit(solution)/shard_map/input_grad_rows/ppermute | solution.py:376
  (24 other events, 256.1 us)
